TPU v7x, 512 devices: a whole 4x8x8 slice. The times are simulated.
512 devices in a mesh: tile: 32 (over z, y_lo, core), scan: 16 (over x, y_hi).
Axes of the slice: x: 4, y: 8 (y_hi: 4, y_lo: 2; y = y_hi * 2 + y_lo), z: 8, core: 2. Of those that a mesh axis runs over, the one named last changes fastest.
Arguments:
- object_tiles: float32 [2, 384, 8192], P(None, None, 'tile'), may hold values from -6 to 6
- probe_modes: bfloat16 [2, 4, 256, 256], replicated, may hold values from -3 to 3
- amplitudes: bfloat16 [32, 16, 5, 256, 256], P('tile', 'scan'), may hold values from 0 to 3
- row_offsets: int32 [32, 16, 5], P('tile', 'scan'), may hold values from 0 to 128
- col_offsets: int32 [32, 16, 5], P('tile', 'scan'), may hold values from 0 to 255
- slot_counts: int32 [32, 16], P('tile', 'scan'), may hold values from 0 to 5, as said below
Outputs:
- new_object: float32 [2, 384, 8192], P(None, None, 'tile')
- new_probe: float32 [2, 4, 256, 256], replicated
Inputs may be any that keep to these rules, and one draw needn't show every extreme that they name: `slot_counts`: in every row of tiles the counts sum to 32, and one device of each row holds 5 positions.
All inputs are finite; a program needn't handle non-finite values.
Results may differ from a plain program's by a relative error of at most 0.00075.
The roundings to bfloat16 on the way count: a program that leaves them out, or rounds other values in their place, can miss the bound.
Values may be sent and summed in bfloat16 or wider, within the bound.
A program may use at most 64 MiB of HBM per device.

v0:
```python
import math

import jax
import jax.numpy as jnp
from jax import lax
from jax.sharding import PartitionSpec as P

object_step = 0.1
probe_scale = 0.5


def shifted(block, axis, distance):
    devices = range(lax.axis_size(axis))
    route = [(i - distance, i) for i in devices if i - distance in devices]
    return lax.ppermute(block, axis, route)


def dft_tables(extent):
    index = jnp.arange(extent, dtype=jnp.int32)
    phase = index[:, None] * index[None, :] % extent
    angle = phase.astype(jnp.float32) * (2.0 * math.pi / extent)
    factor = 1.0 / math.sqrt(extent)
    return (
        (jnp.cos(angle) * factor).astype(jnp.bfloat16),
        (-jnp.sin(angle) * factor).astype(jnp.bfloat16),
    )


def left_apply(mat_real, mat_imag, val_real, val_imag):
    out_real = jnp.einsum(
        "kl,mlj->mkj", mat_real, val_real, preferred_element_type=jnp.float32
    ) - jnp.einsum("kl,mlj->mkj", mat_imag, val_imag, preferred_element_type=jnp.float32)
    out_imag = jnp.einsum(
        "kl,mlj->mkj", mat_real, val_imag, preferred_element_type=jnp.float32
    ) + jnp.einsum("kl,mlj->mkj", mat_imag, val_real, preferred_element_type=jnp.float32)
    return (out_real, out_imag)


def right_apply(val_real, val_imag, mat_real, mat_imag):
    out_real = jnp.einsum(
        "mkl,lj->mkj", val_real, mat_real, preferred_element_type=jnp.float32
    ) - jnp.einsum("mkl,lj->mkj", val_imag, mat_imag, preferred_element_type=jnp.float32)
    out_imag = jnp.einsum(
        "mkl,lj->mkj", val_imag, mat_real, preferred_element_type=jnp.float32
    ) + jnp.einsum("mkl,lj->mkj", val_real, mat_imag, preferred_element_type=jnp.float32)
    return (out_real, out_imag)


def position_terms(prb_real, prb_imag, patch_real, patch_imag, amplitude, dft_real, dft_imag):
    psi_real = (prb_real * patch_real - prb_imag * patch_imag).astype(jnp.bfloat16)
    psi_imag = (prb_real * patch_imag + prb_imag * patch_real).astype(jnp.bfloat16)
    a_real, a_imag = left_apply(dft_real, dft_imag, psi_real, psi_imag)
    f_real, f_imag = right_apply(
        a_real.astype(jnp.bfloat16), a_imag.astype(jnp.bfloat16), dft_real, dft_imag
    )
    intensity = jnp.sum(f_real * f_real + f_imag * f_imag, axis=0)
    factor = amplitude.astype(jnp.float32) / jnp.sqrt(intensity + 1.0) - 1.0
    d_real = (f_real * factor).astype(jnp.bfloat16)
    d_imag = (f_imag * factor).astype(jnp.bfloat16)
    b_real, b_imag = left_apply(dft_real, -dft_imag, d_real, d_imag)
    e_real, e_imag = right_apply(
        b_real.astype(jnp.bfloat16), b_imag.astype(jnp.bfloat16), dft_real, -dft_imag
    )
    obj_real = jnp.sum(prb_real * e_real + prb_imag * e_imag, axis=0)
    obj_imag = jnp.sum(prb_real * e_imag - prb_imag * e_real, axis=0)
    grad_real = patch_real * e_real + patch_imag * e_imag
    grad_imag = patch_real * e_imag - patch_imag * e_real
    return (jnp.stack([obj_real, obj_imag]), jnp.stack([grad_real, grad_imag]))


def on_device(object_tiles, probe_modes, amplitudes, row_offsets, col_offsets, slot_counts):
    height = object_tiles.shape[1]
    tile_w = object_tiles.shape[2]
    extent = probe_modes.shape[2]
    dft_real, dft_imag = dft_tables(extent)
    probe_f = probe_modes.astype(jnp.float32)
    neighbour = shifted(object_tiles, "tile", -1)
    extended = jnp.concatenate([object_tiles, neighbour], axis=2)
    start_grad = (
        jnp.zeros((2, height, 2 * tile_w), jnp.float32),
        jnp.zeros(probe_modes.shape, jnp.float32),
    )

    def accumulate(carry, amplitude, row_at, col_at):
        obj_grad, probe_grad = carry
        zero_at = jnp.zeros((), jnp.int32)
        patch_cells = lax.dynamic_slice(extended, (zero_at, row_at, col_at), (2, extent, extent))
        obj_term, probe_term = position_terms(
            probe_f[0], probe_f[1], patch_cells[0], patch_cells[1], amplitude, dft_real, dft_imag
        )
        current = lax.dynamic_slice(obj_grad, (zero_at, row_at, col_at), (2, extent, extent))
        obj_grad = lax.dynamic_update_slice(obj_grad, current + obj_term, (zero_at, row_at, col_at))
        return (obj_grad, probe_grad + probe_term)

    def advance(item, carry):
        return accumulate(
            carry, amplitudes[0, 0, item], row_offsets[0, 0, item], col_offsets[0, 0, item]
        )

    obj_grad, probe_grad = lax.fori_loop(0, slot_counts[0, 0], advance, start_grad)
    summed = lax.psum(obj_grad, "scan")
    carried = shifted(summed[:, :, tile_w:], "tile", 1)
    update = summed[:, :, :tile_w] + carried
    new_object = object_tiles + object_step * update
    factor = probe_scale / math.sqrt(lax.axis_size("tile") * lax.axis_size("scan"))
    summed_probe = lax.psum(probe_grad, ("tile", "scan"))
    new_probe = probe_f + factor * summed_probe
    return (new_object, new_probe)


def solution(mesh):
    placed = (
        P(None, None, "tile"),
        P(),
        P("tile", "scan", None, None, None),
        P("tile", "scan", None),
        P("tile", "scan", None),
        P("tile", "scan"),
    )
    return jax.shard_map(
        on_device,
        mesh=mesh,
        in_specs=placed,
        out_specs=(P(None, None, "tile"), P()),
        check_vma=False,
    )
```

profile of v0, /device:TPU:1, one launch (start us, length us, event | category | flops | bytes accessed | tf_op | source)
XLA Modules:
  0.0 716.5 jit_solution(9268009421893233004)
XLA Ops:
  7.2 0.0 copy-start.1
  7.2 0.0 all-reduce.3.cloned.1.call-start
  7.2 8.9 %collective-permute-start = (f32[2,384,256]{2,1,0:T(8,128)}, f32[2,384,256]{2,1,0:T(8,128)}, u32[]{:S(2)}, u32[]{:S(2)}) collective-permute-start(f32[2,384,256]{2,1,0:T(8,128)} %param.8), channel_id=1, source_target_pairs={{16,0},{32,16},{48,32},{64,48},{80,64},{96,80},{112,96},{128,112},... | collective-permute-start | bytes 2359304 | tf_op jit(solution)/shard_map/ppermute | solution.py:15
  16.1 1.4 convert_element_type.143
  17.5 4.4 collective-permute-done
  21.9 0.0 copy-done.1
  21.9 2.5 pad_maximum_fusion
  24.4 0.0 copy-start.3
  24.4 0.0 copy-start.4
  24.4 1.4 broadcast_in_dim.4
  25.8 1.5 broadcast_in_dim.5
  27.3 0.0 copy-done.3
  27.3 0.0 copy-done.4
  27.3 42.1 %while.16 = (s32[]{:T(128)}, f32[2,384,512]{2,1,0:T(8,128)}, f32[2,4,256,256]{3,2,1,0:T(8,128)}, s32[]{:T(128)}, s32[1,1,5]{2,1,0:T(1,128)S(1)}, /*index=5*/s32[...) while((s32[]{:T(128)}, f32[2,384,512]{2,1,0:T(8,128)}, ...), condition=%wide.region_4.5_spmd.clone.clone, body=%wide.region_0.4_spmd.clone.clone.sunk | while | flops 2179006464 | bytes 55443764 | solution.py:100
  27.9 0.7 constant_dynamic-slice_fusion.3
  32.4 1.3 dynamic-slice_bitcast_fusion.3
  33.8 0.3 fusion.223
  34.1 1.2 fusion.224
  35.3 1.3 fusion.225
  36.6 1.2 fusion.227
  37.8 1.3 fusion.228
  39.1 1.3 fusion.229
  40.4 1.3 fusion.226
  41.6 1.3 convolution_subtract_fusion.5
  42.9 1.3 add_reduce_fusion.2
  44.2 1.0 fusion.230
  45.2 1.3 fusion.234
  46.4 1.3 fusion.235
  47.7 1.3 fusion.231
  49.0 1.3 fusion.232
  50.3 1.3 fusion.233
  51.5 1.3 convolution_add_fusion.5
  52.8 1.3 fusion.236
  54.1 2.9 add_bitcast_fusion.2
  57.0 2.2 maximum_add_fusion.4
  59.2 6.1 dynamic_update_slice.9
  65.3 3.4 maximum_add_fusion.5
  69.4 0.0 all-reduce.3.cloned.1.call-update
  69.4 0.0 copy-start
  69.4 0.0 all-reduce.5.cloned.1.call-start
  69.5 0.7 all-reduce.5.cloned.1.call-update
  70.2 340.2 %all-reduce.3.cloned.1.call-done = f32[2,384,512]{2,1,0:T(8,128)} async-done(((f32[2,384,512]{2,1,0:T(8,128)}), f32[2,384,512]{2,1,0:T(8,128)}) %all-reduce.3.cloned.1.call-update) | async-done | bytes 1572880 | tf_op jit(solution)/shard_map/psum | solution.py:101
  410.4 1.2 slice.41
  411.6 0.0 copy-start.2
  411.6 11.7 %collective-permute-start.1 = (f32[2,384,256]{2,1,0:T(8,128)S(1)}, f32[2,384,256]{2,1,0:T(8,128)}, u32[]{:S(2)}, u32[]{:S(2)}) collective-permute-start(f32[2,384,256]{2,1,0:T(8,128)S(1)} %slice.41), channel_id=1, source_target_pairs={{0,16},{16,32},{32,48},{48,64},{64,80},{80,96},{96,112},{112,128},... | collective-permute-start | bytes 2359304 | tf_op jit(solution)/shard_map/ppermute | solution.py:15
  423.3 280.7 %all-reduce.5.cloned.1.call-done = f32[2,4,256,256]{3,2,1,0:T(8,128)} async-done(((f32[2,4,256,256]{3,2,1,0:T(8,128)}), f32[2,4,256,256]{3,2,1,0:T(8,128)}) %all-reduce.5.cloned.1.call-update) | async-done | bytes 2097168 | tf_op jit(solution)/shard_map/psum | solution.py:106
  704.1 0.0 copy-done
  704.1 3.2 multiply_add_fusion
  707.2 0.0 collective-permute-done.1
  707.2 0.0 copy-done.2
  707.2 2.4 fusion.140
Async XLA Ops:
  7.2 14.8 %copy-start.1 = (f32[2,384,256]{2,1,0:T(8,128)S(1)}, f32[2,384,256]{2,1,0:T(8,128)}, u32[]{:S(2)}) copy-start(f32[2,384,256]{2,1,0:T(8,128)} %param.8) | copy-start | bytes 2359300
  7.2 403.2 %all-reduce.3.cloned.1.call-start = ((), (), s32[]{:S(2)}) async-start(), calls=%async_computation | async-start | bytes 3145728 | tf_op jit(solution)/shard_map/psum | solution.py:101
  7.2 14.7 %collective-permute-start = (f32[2,384,256]{2,1,0:T(8,128)}, f32[2,384,256]{2,1,0:T(8,128)}, u32[]{:S(2)}, u32[]{:S(2)}) collective-permute-start(f32[2,384,256]{2,1,0:T(8,128)} %param.8), channel_id=1, source_target_pairs={{16,0},{32,16},{48,32},{64,48},{80,64},{96,80},{112,96},{128,112},... | collective-permute-start | bytes 2359304 | tf_op jit(solution)/shard_map/ppermute | solution.py:15
  24.4 2.9 copy-start.3
  24.4 2.9 copy-start.4
  69.4 634.7 %copy-start = (bf16[2,4,256,256]{3,2,1,0:T(8,128)(2,1)S(1)}, bf16[2,4,256,256]{3,2,1,0:T(8,128)(2,1)}, u32[]{:S(2)}) copy-start(bf16[2,4,256,256]{3,2,1,0:T(8,128)(2,1)} %param.9) | copy-start | bytes 3145732
  69.4 634.7 %all-reduce.5.cloned.1.call-start = ((), (), s32[]{:S(2)}) async-start(), calls=%async_computation.1 | async-start | bytes 4194304 | tf_op jit(solution)/shard_map/psum | solution.py:106
  411.6 295.7 %copy-start.2 = (f32[2,384,256]{2,1,0:T(8,128)S(1)}, f32[2,384,256]{2,1,0:T(8,128)}, u32[]{:S(2)}) copy-start(f32[2,384,256]{2,1,0:T(8,128)} %param.8) | copy-start | bytes 2359300
  411.6 295.7 %collective-permute-start.1 = (f32[2,384,256]{2,1,0:T(8,128)S(1)}, f32[2,384,256]{2,1,0:T(8,128)}, u32[]{:S(2)}, u32[]{:S(2)}) collective-permute-start(f32[2,384,256]{2,1,0:T(8,128)S(1)} %slice.41), channel_id=1, source_target_pairs={{0,16},{16,32},{32,48},{48,64},{64,80},{80,96},{96,112},{112,128},... | collective-permute-start | bytes 2359304 | tf_op jit(solution)/shard_map/ppermute | solution.py:15
Sparse Core Ops, SparseCore 0:
  69.5 340.8 all-reduce.2
  415.9 288.1 all-reduce.4
where the time goes:
time: 719 us; the launch traced here: 716 us
  waiting for transfers between devices  626 us (87%)
  matrix products  21.9 us (3%)
  starting transfers between devices  20.7 us (3%)
  other arithmetic  16.3 us (2%)
  between operations  14.1 us (2%)
  local copies, waits for them, and re-layouts  12.2 us (2%)
    psum x1, waiting for transfers between devices, on_device(): summed = lax.psum(obj_grad, 'scan')  340 us
    psum x1, waiting for transfers between devices, on_device(): summed_probe = lax.psum(probe_grad, ('tile', 'scan'))  281 us
    ppermute x2, starting transfers between devices, shifted(): return lax.ppermute(block, axis, route)  20.6 us
  transfers between devices with their start and end apart: 4, of which 3 were waited for; matrix products, arithmetic and copies ran while one was open for 1% of the time, Pallas kernels for 0%

commit v1 on v0

v1 whole, which is shorter than its diff:
```python
import functools
import math

import jax
import jax.numpy as jnp
import numpy as np
from jax import lax
from jax.experimental import pallas as pl
from jax.experimental.pallas import tpu as pltpu
from jax.sharding import PartitionSpec as P

F32, BF16 = jnp.float32, jnp.bfloat16
MESH = pl.DeviceIdType.MESH
KEEP = 2
SIZES = (8, 2, 2, 4, 4)
object_step = 0.1
probe_scale = 0.5


def dft_tables(extent):
    index = np.arange(extent)
    angle = (index[:, None] * index[None, :] % extent) * (2.0 * math.pi / extent)
    factor = 1.0 / math.sqrt(extent)
    table = np.stack([np.cos(angle) * factor, -np.sin(angle) * factor])
    return jnp.asarray(table.astype(np.float32)).astype(BF16)


def rows_loop(total, step, body):
    def trip(i, carry):
        body(pl.multiple_of(i * step, step))
        return carry
    lax.fori_loop(0, total // step, trip, 0)


def dot(a, b):
    return jnp.dot(a, b, preferred_element_type=F32)


def positions_kernel(mine, others, tile, halo, probe, amp_own, amp_got, table,
                     grad_out, prb_out,
                     amp, lanes, patch, stack, side, wide, term, forward, inverse, arrived):
    n = probe.shape[2]
    modes = probe.shape[1]
    height, tw = tile.shape[1], tile.shape[2]
    tall = n + 8
    edge = mine[3, 0] > 0

    def clear(at):
        grad_out[:, :, pl.ds(at, 8), :] = jnp.zeros((2, 2, 8, tw), F32)
    rows_loop(height, 8, clear)

    def clear_probe(at):
        prb_out[:, :, pl.ds(at, 8), :] = jnp.zeros((2, modes, 8, n), F32)
    rows_loop(n, 8, clear_probe)

    forward[:n, :n] = table[0]
    forward[n:, n:] = table[0]
    forward[n:, :n] = table[1]
    forward[:n, n:] = -table[1]
    inverse[:n, :n] = table[0]
    inverse[n:, n:] = table[0]
    inverse[n:, :n] = -table[1]
    inverse[:n, n:] = table[1]

    def position(r, c):
        base = pl.multiple_of(jnp.minimum(r // 8 * 8, height - tall), 8)
        rem = r - base
        back_r = tall - rem
        back_c = lax.rem(2 * tw - c, 2 * tw)

        def lane_in(at):
            rows = pl.ds(pl.multiple_of(base + at, 8), 24)
            for p in range(2):
                beside = jnp.where(edge, 0.0, halo[p, rows, :])
                x = jnp.concatenate([tile[p, rows, :], beside], 1)
                lanes[p, pl.ds(at, 24), :] = pltpu.roll(x, back_c, 1)[:, :n]
        rows_loop(tall, 24, lane_in)
        for p in range(2):
            for h in range(n // 128):
                cols = pl.ds(h * 128, 128)
                patch[p, :, cols] = pltpu.roll(lanes[p, :, cols], back_r, 0)[:n]

        def make_psi(at):
            rows, low = pl.ds(at, 16), pl.ds(pl.multiple_of(at + n, 16), 16)
            xr, xi = patch[0, rows, :], patch[1, rows, :]
            for m in range(modes):
                pr = probe[0, m, rows, :].astype(F32)
                pi = probe[1, m, rows, :].astype(F32)
                stack[m, rows, :] = (pr * xr - pi * xi).astype(BF16)
                stack[m, low, :] = (pr * xi + pi * xr).astype(BF16)
        rows_loop(n, 16, make_psi)

        for m in range(modes):
            a = dot(forward[...], stack[m]).astype(BF16)
            side[m, :, :n] = a[:n]
            side[m, :, n:] = a[n:]
        for m in range(modes):
            wide[m] = dot(side[m], inverse[...])

        pltpu.make_async_copy(amp_own.at[0], amp, arrived).wait()

        def make_d(at):
            rows, low = pl.ds(at, 16), pl.ds(pl.multiple_of(at + n, 16), 16)
            total = jnp.zeros((16, n), F32)
            for m in range(modes):
                fr, fi = wide[m, rows, :n], wide[m, rows, n:]
                total += fr * fr + fi * fi
            factor = amp[rows, :].astype(F32) / jnp.sqrt(total + 1.0) - 1.0
            for m in range(modes):
                stack[m, rows, :] = (wide[m, rows, :n] * factor).astype(BF16)
                stack[m, low, :] = (wide[m, rows, n:] * factor).astype(BF16)
        rows_loop(n, 16, make_d)

        for m in range(modes):
            b = dot(inverse[...], stack[m]).astype(BF16)
            side[m, :, :n] = b[:n]
            side[m, :, n:] = b[n:]
        for m in range(modes):
            wide[m] = dot(side[m], forward[...])

        def finish(at):
            rows = pl.ds(at, 16)
            xr, xi = patch[0, rows, :], patch[1, rows, :]
            tr = jnp.zeros((16, n), F32)
            ti = jnp.zeros((16, n), F32)
            for m in range(modes):
                er, ei = wide[m, rows, :n], wide[m, rows, n:]
                pr = probe[0, m, rows, :].astype(F32)
                pi = probe[1, m, rows, :].astype(F32)
                tr += pr * er + pi * ei
                ti += pr * ei - pi * er
                prb_out[0, m, rows, :] += xr * er + xi * ei
                prb_out[1, m, rows, :] += xr * ei - xi * er
            term[0, rows, :] = tr
            term[1, rows, :] = ti
        rows_loop(n, 16, finish)

        term[:, n:, :] = jnp.zeros((2, 8, n), F32)
        for p in range(2):
            for h in range(n // 128):
                cols = pl.ds(h * 128, 128)
                lanes[p, :, cols] = pltpu.roll(term[p, :, cols], rem, 0)

        def lane_out(at):
            rows = pl.ds(pl.multiple_of(base + at, 8), 24)
            for p in range(2):
                y = lanes[p, pl.ds(at, 24), :]
                y = pltpu.roll(jnp.concatenate([y, jnp.zeros_like(y)], 1), c, 1)
                grad_out[0, p, rows, :] += y[:, :tw]
                grad_out[1, p, rows, :] += y[:, tw:]
        rows_loop(tall, 24, lane_out)

    slots = KEEP + amp_got.shape[0]

    def item_trip(item, carry):
        own = item < KEEP
        other = jnp.maximum(item - KEEP, 0)
        r = jnp.where(own, mine[0, item], others[other, 0, item])
        c = jnp.where(own, mine[1, item], others[other, 1, item])
        count = jnp.where(own, mine[2, item], others[other, 2, item])

        @pl.when(item < count)
        def _():
            @pl.when(own)
            def _():
                pltpu.make_async_copy(amp_own.at[item], amp, arrived).start()

            @pl.when(jnp.logical_not(own))
            def _():
                pltpu.make_async_copy(amp_got.at[other], amp, arrived).start()
            position(r, c)
        return carry
    lax.fori_loop(0, slots, item_trip, 0)

    @pl.when(edge)
    def _():
        def drop(at):
            grad_out[1, :, pl.ds(at, 8), :] = jnp.zeros((2, 8, tw), F32)
        rows_loop(height, 8, drop)


def positions(mine, others, tile, halo, probe, amp_own, amp_got, table):
    _, modes, n, _ = probe.shape
    height, tw = tile.shape[1:]
    vmem, smem = pl.BlockSpec(memory_space=pltpu.VMEM), pl.BlockSpec(memory_space=pltpu.SMEM)
    anywhere = pl.BlockSpec(memory_space=pl.ANY)
    return pl.pallas_call(
        positions_kernel,
        out_shape=(
            jax.ShapeDtypeStruct((2, 2, height, tw), F32),
            jax.ShapeDtypeStruct((2, modes, n, n), F32),
        ),
        in_specs=[smem, smem, vmem, vmem, vmem, anywhere, anywhere, vmem],
        out_specs=(vmem, vmem),
        scratch_shapes=[
            pltpu.VMEM((n, n), BF16),
            pltpu.VMEM((2, n + 8, n), F32),
            pltpu.VMEM((2, n, n), F32),
            pltpu.VMEM((modes, 2 * n, n), BF16),
            pltpu.VMEM((modes, n, 2 * n), BF16),
            pltpu.VMEM((modes, n, 2 * n), F32),
            pltpu.VMEM((2, n + 8, n), F32),
            pltpu.VMEM((2 * n, 2 * n), BF16),
            pltpu.VMEM((2 * n, 2 * n), BF16),
            pltpu.SemaphoreType.DMA,
        ],
        compiler_params=pltpu.CompilerParams(vmem_limit_bytes=48 << 20),
        name="positions",
    )(mine, others, tile, halo, probe, amp_own, amp_got, table)


class Place:
    def __init__(self, sizes):
        self.nz, self.nlo, self.nc, self.nx, self.nhi = sizes
        self.ny = self.nlo * self.nhi
        self.tiles, self.scans = self.nz * self.nlo * self.nc, self.nx * self.nhi
        self.t, self.s = lax.axis_index("tile"), lax.axis_index("scan")
        self.core = lax.rem(self.t, self.nc)
        self.lo = lax.rem(self.t // self.nc, self.nlo)
        self.z = self.t // (self.nc * self.nlo)
        self.x, self.hi = self.s // self.nhi, lax.rem(self.s, self.nhi)
        self.y = self.hi * self.nlo + self.lo

    def device(self, z, y, core, x):
        lo, hi = lax.rem(y, self.nlo), y // self.nlo
        return {"tile": (z * self.nlo + lo) * self.nc + core, "scan": x * self.nhi + hi}

    def along_z(self, d):
        at = lax.rem(self.z + d, self.nz)
        return at, self.device(at, self.y, self.core, self.x)

    def along_y(self, d):
        at = lax.rem(self.y + d, self.ny)
        return at, self.device(self.z, at, self.core, self.x)

    def along_hi(self, d):
        at = lax.rem(self.hi + d, self.nhi)
        return at, self.device(self.z, at * self.nlo + self.lo, self.core, self.x)

    def along_x(self, d):
        at = lax.rem(self.x + d, self.nx)
        return at, self.device(self.z, self.y, self.core, at)

    def tile(self, d):
        return {"tile": lax.rem(self.t + self.tiles + d, self.tiles), "scan": self.s}

    def partner(self):
        return self.device(self.z, self.y, 1 - self.core, self.x)


def greet(devices):
    barrier = pltpu.get_barrier_semaphore()
    for device in devices:
        pl.semaphore_signal(barrier, inc=1, device_id=device, device_id_type=MESH)
    pl.semaphore_wait(barrier, len(devices))


def sums_kernel(sizes, grad, prb, upd_out, prb_out,
                near, quarter, near2, slim, shifted,
                give, got, mixed, first, held, second, small, third,
                send, recv):
    at = Place(sizes)
    used = [0]
    started = []

    def copy(src, dst, device):
        k = used[0]
        used[0] += 1
        c = pltpu.make_async_remote_copy(
            src_ref=src, dst_ref=dst, send_sem=send.at[k], recv_sem=recv.at[k],
            device_id=device, device_id_type=MESH)
        c.start()
        started.append(c)
        return c

    greet([at.partner(), at.tile(1), at.tile(-1)]
          + [at.along_z(d)[1] for d in range(1, at.nz)]
          + [at.along_y(d)[1] for d in range(1, at.ny)]
          + [at.along_x(d)[1] for d in range(1, at.nx)])

    height, width = grad.shape[1], grad.shape[2]
    xrows = height // at.nx
    hrows = xrows // at.nhi
    total = prb.shape[0]
    half = total // 2
    quart = half // 2

    def block(index, rows):
        return pl.ds(pl.multiple_of(index * rows, 8), rows)

    other_base = (1 - at.core) * half
    my_base = at.core * half

    def cast_half(r):
        give[pl.ds(r, 32), :] = prb[pl.ds(pl.multiple_of(other_base + r, 8), 32), :].astype(BF16)
    rows_loop(half, 32, cast_half)
    p0 = copy(give, got, at.partner())

    o1 = []
    for d in range(1, at.nx):
        to, device = at.along_x(d)
        o1.append(copy(grad.at[:, block(to, xrows), :], near.at[d - 1], device))

    p0.wait_recv()

    def mix(r):
        rows = pl.ds(r, 32)
        mine = prb[pl.ds(pl.multiple_of(my_base + r, 8), 32), :]
        mixed[rows, :] = (mine + got[rows, :].astype(F32)).astype(BF16)
    rows_loop(half, 32, mix)

    axes = ((at.along_z, at.along_y, at.nz, at.ny, at.z, at.y),
            (at.along_y, at.along_z, at.ny, at.nz, at.y, at.z))
    p1 = [[], []]
    for d in range(1, max(at.nz, at.ny)):
        for h, (one, _, n1, n2, c1, c2) in enumerate(axes):
            if d < n1:
                to, device = one(d)
                rows = quart // n1
                src = mixed.at[pl.ds(pl.multiple_of(h * quart + to * rows, 16), rows), :]
                p1[h].append(copy(src, first.at[h, d - 1, pl.ds(0, rows), :], device))

    p2 = [[], []]
    for h, (_, two, n1, n2, c1, c2) in enumerate(axes):
        rows = quart // n1
        for c in p1[h]:
            c.wait_recv()
        base = h * quart + c1 * rows

        def add_first(r, h=h, n1=n1, base=base):
            acc = (prb[pl.ds(pl.multiple_of(my_base + base + r, 8), 16), :]
                   + got[pl.ds(pl.multiple_of(base + r, 16), 16), :].astype(F32))
            for d in range(n1 - 1):
                acc += first[h, d, pl.ds(r, 16), :].astype(F32)
            held[h, pl.ds(r, 16), :] = acc
        rows_loop(rows, 16, add_first)
        sub = rows // n2
        for d in range(1, n2):
            to, device = two(d)
            p2[h].append(copy(held.at[h, block(to, sub), :], second.at[h, d - 1], device))

    for c in o1:
        c.wait_recv()
    xbase = at.x * xrows

    def add_near(r):
        rows = pl.ds(r, 8)
        for k in range(2):
            acc = grad[k, pl.ds(pl.multiple_of(xbase + r, 8), 8), :]
            for d in range(at.nx - 1):
                acc += near[d, k, rows, :]
            quarter[k, rows, :] = acc
    rows_loop(xrows, 8, add_near)
    o2 = []
    for d in range(1, at.nhi):
        to, device = at.along_hi(d)
        o2.append(copy(quarter.at[:, block(to, hrows), :], near2.at[d - 1], device))

    sub = quart // (at.nz * at.ny)
    for h, (_, _, n1, n2, c1, c2) in enumerate(axes):
        for c in p2[h]:
            c.wait_recv()
        acc = held[h, block(c2, sub), :]
        for d in range(n2 - 1):
            acc += second[h, d]
        small[h] = acc
        third[at.x, h] = acc
    p3 = []
    for d in range(1, at.nx):
        _, device = at.along_x(d)
        p3.append(copy(small, third.at[at.x], device))
    for c in p3:
        c.wait_recv()
    p4 = [[], []]
    for h, (_, two, n1, n2, c1, c2) in enumerate(axes):
        acc = third[0, h]
        for k in range(1, at.nx):
            acc += third[k, h]
        rows = pl.ds(pl.multiple_of(my_base + h * quart + c1 * (quart // n1) + c2 * sub, 8), sub)
        prb_out[rows, :] = acc
        for d in range(1, n2):
            p4[h].append(copy(prb_out.at[rows, :], prb_out.at[rows, :], two(d)[1]))

    for c in o2:
        c.wait_recv()
    hbase = at.hi * hrows

    def add_near2(r):
        rows = pl.ds(r, 8)
        for k in (1, 0):
            acc = quarter[k, pl.ds(pl.multiple_of(hbase + r, 8), 8), :]
            for d in range(at.nhi - 1):
                acc += near2[d, k, rows, :]
            slim[k, rows, :] = acc
    rows_loop(hrows, 8, add_near2)
    o0 = copy(slim.at[1], shifted, at.tile(1))

    p5 = [[], []]
    for h, (one, _, n1, n2, c1, c2) in enumerate(axes):
        for c in p4[h]:
            c.wait_recv()
        rows = pl.ds(pl.multiple_of(my_base + h * quart + c1 * (quart // n1), 8), quart // n1)
        for d in range(1, n1):
            p5[h].append(copy(prb_out.at[rows, :], prb_out.at[rows, :], one(d)[1]))

    o0.wait_recv()
    obase = xbase + hbase

    def finish(r):
        upd_out[pl.ds(pl.multiple_of(obase + r, 8), 8), :] = slim[0, pl.ds(r, 8), :] + shifted[pl.ds(r, 8), :]
    rows_loop(hrows, 8, finish)
    o3 = []
    orow = pl.ds(pl.multiple_of(obase, 8), hrows)
    for d in range(1, at.nhi):
        o3.append(copy(upd_out.at[orow, :], upd_out.at[orow, :], at.along_hi(d)[1]))

    p6 = []
    for h, (one, _, n1, n2, c1, c2) in enumerate(axes):
        rows = pl.ds(pl.multiple_of(my_base + h * quart + c1 * (quart // n1), 8), quart // n1)
        p6.append(copy(prb_out.at[rows, :], prb_out.at[rows, :], at.partner()))

    for c in o3:
        c.wait_recv()
    o4 = []
    xrow = pl.ds(pl.multiple_of(xbase, 8), xrows)
    for d in range(1, at.nx):
        o4.append(copy(upd_out.at[xrow, :], upd_out.at[xrow, :], at.along_x(d)[1]))

    for d in range(1, max(at.nz, at.ny)):
        for h, (_, _, n1, n2, c1, c2) in enumerate(axes):
            if d < n1:
                p5[h][d - 1].wait_recv()
                origin = lax.rem(c1 + n1 - d, n1)
                rows = pl.ds(pl.multiple_of(my_base + h * quart + origin * (quart // n1), 8), quart // n1)
                p6.append(copy(prb_out.at[rows, :], prb_out.at[rows, :], at.partner()))
    for c in o4:
        c.wait_recv()
    for c in p6:
        c.wait_recv()
    for c in started:
        c.wait_send()


def count_copies(sizes):
    nz, nlo, nc, nx, nhi = sizes
    ny = nlo * nhi
    return 2 + 2 * (nx - 1) + 2 * (nhi - 1) + 4 * (nz - 1 + ny - 1) + (nx - 1) + (nz + ny)


def sums(sizes, grad, prb):
    nz, nlo, nc, nx, nhi = sizes
    ny = nlo * nhi
    height, width = grad.shape[1:]
    total, pw = prb.shape
    xrows, hrows = height // nx, height // nx // nhi
    half, quart = total // 2, total // 4
    n1, small_n = max(nz, ny), min(nz, ny)
    sub = quart // (nz * ny)
    vmem = pl.BlockSpec(memory_space=pltpu.VMEM)
    copies = count_copies(sizes)
    return pl.pallas_call(
        functools.partial(sums_kernel, sizes),
        out_shape=(jax.ShapeDtypeStruct((height, width), F32), jax.ShapeDtypeStruct((total, pw), F32)),
        in_specs=[vmem, vmem],
        out_specs=(vmem, vmem),
        scratch_shapes=[
            pltpu.VMEM((nx - 1, 2, xrows, width), F32),
            pltpu.VMEM((2, xrows, width), F32),
            pltpu.VMEM((nhi - 1, 2, hrows, width), F32),
            pltpu.VMEM((2, hrows, width), F32),
            pltpu.VMEM((hrows, width), F32),
            pltpu.VMEM((half, pw), BF16),
            pltpu.VMEM((half, pw), BF16),
            pltpu.VMEM((half, pw), BF16),
            pltpu.VMEM((2, n1 - 1, quart // small_n, pw), BF16),
            pltpu.VMEM((2, quart // small_n, pw), F32),
            pltpu.VMEM((2, n1 - 1, sub, pw), F32),
            pltpu.VMEM((2, sub, pw), F32),
            pltpu.VMEM((nx, 2, sub, pw), F32),
            pltpu.SemaphoreType.DMA((copies,)),
            pltpu.SemaphoreType.DMA((copies,)),
        ],
        compiler_params=pltpu.CompilerParams(
            collective_id=1, has_side_effects=True, vmem_limit_bytes=48 << 20),
        name="sums",
    )(grad, prb)


def spread_kernel(sizes, tile, amp, meta, halo, amp_got, meta_got, send, recv):
    at = Place(sizes)
    keep = amp.shape[0] - amp_got.shape[0]
    moved = amp_got.shape[0]
    devices = [at.along_x(d)[1] for d in range(1, moved + 1)]
    greet([at.tile(1), at.tile(-1)] + devices)
    copies = []

    def copy(src, dst, device):
        k = len(copies)
        c = pltpu.make_async_remote_copy(
            src_ref=src, dst_ref=dst, send_sem=send.at[k], recv_sem=recv.at[k],
            device_id=device, device_id_type=MESH)
        c.start()
        copies.append(c)

    copy(tile, halo, at.tile(-1))
    for k, device in enumerate(devices):
        copy(meta, meta_got.at[k], device)
        copy(amp.at[keep + k], amp_got.at[k], device)
    for c in copies:
        c.wait()


def spread(sizes, tile, amp, meta, moved):
    anywhere = pl.BlockSpec(memory_space=pl.ANY)
    return pl.pallas_call(
        functools.partial(spread_kernel, sizes),
        out_shape=(
            jax.ShapeDtypeStruct(tile.shape, tile.dtype),
            jax.ShapeDtypeStruct((moved,) + amp.shape[1:], amp.dtype),
            jax.ShapeDtypeStruct((moved,) + meta.shape, meta.dtype),
        ),
        in_specs=[anywhere] * 3,
        out_specs=(anywhere,) * 3,
        scratch_shapes=[pltpu.SemaphoreType.DMA((1 + 2 * moved,))] * 2,
        compiler_params=pltpu.CompilerParams(collective_id=0, has_side_effects=True),
        name="spread",
    )(tile, amp, meta)


def on_device(object_tiles, probe_modes, amplitudes, row_offsets, col_offsets, slot_counts):
    slots = amplitudes.shape[2]
    edge = (lax.axis_index("tile") == lax.axis_size("tile") - 1).astype(jnp.int32)
    pad = ((0, 0), (0, 128 - slots))
    meta = jnp.concatenate([
        jnp.pad(row_offsets[0], pad),
        jnp.pad(col_offsets[0], pad),
        jnp.full((1, 128), slot_counts[0, 0]),
        jnp.full((1, 128), edge),
        jnp.zeros((4, 128), jnp.int32),
    ])
    halo, amp_got, meta_got = spread(SIZES, object_tiles, amplitudes[0, 0], meta, slots - KEEP)
    grad, probe_grad = positions(
        meta, meta_got, object_tiles, halo, probe_modes, amplitudes[0, 0], amp_got,
        dft_tables(probe_modes.shape[2]),
    )
    width = object_tiles.shape[2]
    update, summed = sums(SIZES, grad.reshape(2, -1, width), probe_grad.reshape(-1, probe_modes.shape[3]))
    new_object = object_tiles + object_step * update.reshape(object_tiles.shape)
    factor = probe_scale / math.sqrt(lax.axis_size("tile") * lax.axis_size("scan"))
    new_probe = probe_modes.astype(F32) + factor * summed.reshape(probe_modes.shape)
    return (new_object, new_probe)


def solution(mesh):
    nz, nlo, nc, nx, nhi = SIZES
    if mesh.shape["tile"] != nz * nlo * nc or mesh.shape["scan"] != nx * nhi:
        raise ValueError("other mesh")
    placed = (
        P(None, None, "tile"),
        P(),
        P("tile", "scan", None, None, None),
        P("tile", "scan", None),
        P("tile", "scan", None),
        P("tile", "scan"),
    )
    return jax.shard_map(
        on_device,
        mesh=mesh,
        in_specs=placed,
        out_specs=(P(None, None, "tile"), P()),
        check_vma=False,
    )
```

time: 719 us -> 126 us (0.18)
  waiting for transfers between devices: 626 us -> 0 us
  Pallas kernels: 0 us -> 112 us
  matrix products: 21.9 us -> 0 us
  starting transfers between devices: 20.7 us -> 0 us
  other arithmetic: 16.3 us -> 2.79 us
  between operations: 14.1 us -> 1.47 us
    psum x2 -> x0, waiting for transfers between devices: 621 us -> none  [the longest x1 340 us: on_device(): summed = lax.psum(obj_grad, 'scan')]
    pallas_call x0 -> x3, Pallas kernels: none -> 112 us  [the longest x1 71.4 us: sums(): pl.pallas_call(functools.partial(sums_kernel, sizes), out_shape=(jax.Shap...]
    dot_general x16 -> x0, matrix products: 21.9 us -> none  [the longest x2 4.19 us: right_apply(): jnp.einsum('mkl,lj->mkj', val_imag, mat_imag, preferred_element_type=jnp....]
    ppermute x2 -> x0, starting transfers between devices: 20.6 us -> none  [shifted(): return lax.ppermute(block, axis, route)]
    add x4 -> x2, other arithmetic: 11.2 us -> 2.54 us  [the longest x1 1.56 us: on_device(): probe_modes.astype(F32) + factor * summed.reshape(probe_modes.shape)]
  transfers between devices with their start and end apart: 4 -> 0, of which waited for: 3 -> 0; matrix products, arithmetic and copies ran while one was open for 1% -> 0% of each run, Pallas kernels for 0% -> 0%
where the time goes in v1:
time: 126 us; the launch traced here: 125 us
  Pallas kernels  112 us (89%)
  local copies, waits for them, and re-layouts  8.63 us (7%)
  other arithmetic  2.79 us (2%)
  between operations  1.47 us (1%)
    pallas_call x1, Pallas kernels, sums(): pl.pallas_call(functools.partial(sums_kernel, sizes), out_shape=(jax.Shap...  71.4 us
    pallas_call x1, Pallas kernels, positions(): pl.pallas_call(positions_kernel, out_shape=(jax.ShapeDtypeStruct((2, 2, h...  23.4 us
    pallas_call x1, Pallas kernels, spread(): pl.pallas_call(functools.partial(spread_kernel, sizes), out_shape=(jax.Sh...  16.9 us
    unnamed x18, local copies, waits for them, and re-layouts  6.7 us

profile of v1, /device:TPU:1, one launch (start us, length us, event | category | flops | bytes accessed | tf_op | source)
XLA Modules:
  0.0 124.5 jit_solution(1673970552876804782)
XLA Ops:
  0.6 0.0 copy-start.2
  1.4 0.7 pad.7
  2.1 0.7 pad.8
  2.7 0.6 concatenate.3.meta.mine
  3.3 16.9 %spread.1 = (f32[2,384,256]{2,1,0:T(8,128)}, bf16[3,256,256]{2,1,0:T(8,128)(2,1)}, s32[3,8,128]{2,1,0:T(8,128)}) custom-call(f32[2,384,256]{2,1,0:T(8,128)} %tile.3, bf16[5,256,256]{2,1,0:T(8,128)(2,1)} %bitcast.9, s32[8,128]{1,0:T(8,128)} %concatenate.3.meta.mine), custom_call_target="tpu_custom_call" | custom-call | tf_op jit(solution)/shard_map/spread/pallas_call | solution.py:515
  20.2 0.0 copy-done.2
  20.2 0.0 copy-start
  20.2 1.1 copy-done
  21.4 0.0 copy-start.3
  21.4 1.1 copy-done.3
  22.4 0.0 copy-start.4
  22.5 1.1 copy-done.4
  23.6 0.0 copy-start.5
  23.6 1.0 copy-done.5
  24.6 0.0 copy-start.6
  24.6 0.9 copy-done.6
  25.5 0.0 copy-start.7
  25.5 0.7 copy-done.7
  26.2 0.0 copy-start.8
  26.2 0.7 copy-done.8
  26.9 23.4 %positions.1 = (f32[2,2,384,256]{3,2,1,0:T(8,128)S(1)}, f32[2,4,256,256]{3,2,1,0:T(8,128)}) custom-call(s32[8,128]{1,0:T(8,128)S(1)} %copy-done.7, s32[3,8,128]{2,1,0:T(8,128)S(1)} %copy-done.8, f32[2,384,256]{2,1,0:T(8,128)S(1)} %copy-done, f32[2,384,256]{2,1,0:T(8,128)S(1)} %copy-done.4, bf16[2,4,256,256]{3,2,1,0:T(8,128)(2,1)S(1)} %copy-done.2, ...), custom_call_target="tpu_custom_call" | custom-call | tf_op jit(solution)/shard_map/positions/pallas_call | solution.py:187
  50.3 0.0 copy-start.1
  50.3 71.4 %sums.1 = (f32[768,256]{1,0:T(8,128)S(1)}, f32[2048,256]{1,0:T(8,128)S(1)}) custom-call(f32[2,768,256]{2,1,0:T(8,128)S(1)} %bitcast.11, f32[2048,256]{1,0:T(8,128)} %bitcast.14), custom_call_target="tpu_custom_call" | custom-call | tf_op jit(solution)/shard_map/sums/pallas_call | solution.py:461
  121.7 0.1 broadcast_multiply_fusion.1
  121.8 0.0 copy-done.1
  121.8 1.0 add.10
  122.8 0.2 broadcast_multiply_fusion
  123.0 1.6 %convert_add_fusion = f32[2,4,256,256]{3,2,1,0:T(8,128)} fusion(f32[2,4,256,256]{3,2,1,0:T(8,128)S(1)} %bitcast.12, bf16[2,4,256,256]{3,2,1,0:T(8,128)(2,1)S(1)} %copy-done.2), kind=kLoop, calls=%fused_computation | loop fusion | flops 1048576 | bytes 5242880 | tf_op jit(solution)/shard_map/add | solution.py:550
  (3 shorter events, 0.0 us)
Async XLA Ops:
  0.6 19.6 %copy-start.2 = (bf16[2,4,256,256]{3,2,1,0:T(8,128)(2,1)S(1)}, bf16[2,4,256,256]{3,2,1,0:T(8,128)(2,1)}, u32[]{:S(2)}) copy-start(bf16[2,4,256,256]{3,2,1,0:T(8,128)(2,1)} %probe.1) | copy-start | bytes 3145732
  20.2 1.1 copy-start
  21.4 1.1 copy-start.3
  22.4 1.1 copy-start.4
  23.6 1.0 copy-start.5
  24.6 0.9 copy-start.6
  25.5 0.7 copy-start.7
  26.2 0.7 copy-start.8
  50.3 71.5 %copy-start.1 = (f32[2,384,256]{2,1,0:T(8,128)S(1)}, f32[2,384,256]{2,1,0:T(8,128)}, u32[]{:S(2)}) copy-start(f32[2,384,256]{2,1,0:T(8,128)} %tile.3) | copy-start | bytes 2359300

commit v2 on v1

--- a/solution.py
+++ b/solution.py
@@ -12,6 +12,7 @@
 F32, BF16 = jnp.float32, jnp.bfloat16
 MESH = pl.DeviceIdType.MESH
 KEEP = 2
+COPIES = 96
 SIZES = (8, 2, 2, 4, 4)
 object_step = 0.1
 probe_scale = 0.5
@@ -36,14 +37,26 @@
     return jnp.dot(a, b, preferred_element_type=F32)
 
 
-def positions_kernel(mine, others, tile, halo, probe, amp_own, amp_got, table,
+def positions_kernel(rows_own_in, cols_own_in, count_own_in, rows_got_in, cols_got_in, count_got_in,
+                     tile_in, halo, probe_in, amp_own, amp_got, table_in,
                      grad_out, prb_out,
-                     amp, lanes, patch, stack, side, wide, term, forward, inverse, arrived):
+                     rows_own, cols_own, count_own, rows_got, cols_got, count_got, tile, probe, table,
+                     amp, lanes, patch, stack, side, wide, term, forward, inverse, arrived, loaded):
     n = probe.shape[2]
     modes = probe.shape[1]
+    loads = [
+        pltpu.make_async_copy(src, dst, loaded.at[k])
+        for k, (src, dst) in enumerate([
+            (tile_in, tile), (probe_in, probe), (table_in, table),
+            (rows_own_in, rows_own), (cols_own_in, cols_own), (count_own_in, count_own),
+            (rows_got_in, rows_got), (cols_got_in, cols_got), (count_got_in, count_got),
+        ])
+    ]
+    for load in loads:
+        load.start()
     height, tw = tile.shape[1], tile.shape[2]
     tall = n + 8
-    edge = mine[3, 0] > 0
+    edge = lax.axis_index("tile") == lax.axis_size("tile") - 1
 
     def clear(at):
         grad_out[:, :, pl.ds(at, 8), :] = jnp.zeros((2, 2, 8, tw), F32)
@@ -53,6 +66,8 @@
         prb_out[:, :, pl.ds(at, 8), :] = jnp.zeros((2, modes, 8, n), F32)
     rows_loop(n, 8, clear_probe)
 
+    for load in loads:
+        load.wait()
     forward[:n, :n] = table[0]
     forward[n:, n:] = table[0]
     forward[n:, :n] = table[1]
@@ -155,9 +170,9 @@
     def item_trip(item, carry):
         own = item < KEEP
         other = jnp.maximum(item - KEEP, 0)
-        r = jnp.where(own, mine[0, item], others[other, 0, item])
-        c = jnp.where(own, mine[1, item], others[other, 1, item])
-        count = jnp.where(own, mine[2, item], others[other, 2, item])
+        r = jnp.where(own, rows_own[0, item], rows_got[other, 0, item])
+        c = jnp.where(own, cols_own[0, item], cols_got[other, 0, item])
+        count = jnp.where(own, count_own[0, 0], count_got[other, 0, 0])
 
         @pl.when(item < count)
         def _():
@@ -179,20 +194,23 @@
         rows_loop(height, 8, drop)
 
 
-def positions(mine, others, tile, halo, probe, amp_own, amp_got, table):
+def positions(own, got, tile, halo, probe, amp_own, amp_got, table):
     _, modes, n, _ = probe.shape
     height, tw = tile.shape[1:]
-    vmem, smem = pl.BlockSpec(memory_space=pltpu.VMEM), pl.BlockSpec(memory_space=pltpu.SMEM)
-    anywhere = pl.BlockSpec(memory_space=pl.ANY)
+    vmem, anywhere = pl.BlockSpec(memory_space=pltpu.VMEM), pl.BlockSpec(memory_space=pl.ANY)
+    hbm = pl.BlockSpec(memory_space=pltpu.HBM)
     return pl.pallas_call(
         positions_kernel,
         out_shape=(
             jax.ShapeDtypeStruct((2, 2, height, tw), F32),
             jax.ShapeDtypeStruct((2, modes, n, n), F32),
         ),
-        in_specs=[smem, smem, vmem, vmem, vmem, anywhere, anywhere, vmem],
+        in_specs=[hbm] * 3 + [anywhere] * 3 + [hbm, vmem, hbm, hbm, anywhere, hbm],
         out_specs=(vmem, vmem),
-        scratch_shapes=[
+        scratch_shapes=[pltpu.SMEM(m.shape, m.dtype) for m in (*own, *got)] + [
+            pltpu.VMEM(tile.shape, F32),
+            pltpu.VMEM(probe.shape, BF16),
+            pltpu.VMEM(table.shape, BF16),
             pltpu.VMEM((n, n), BF16),
             pltpu.VMEM((2, n + 8, n), F32),
             pltpu.VMEM((2, n, n), F32),
@@ -203,10 +221,11 @@
             pltpu.VMEM((2 * n, 2 * n), BF16),
             pltpu.VMEM((2 * n, 2 * n), BF16),
             pltpu.SemaphoreType.DMA,
+            pltpu.SemaphoreType.DMA((9,)),
         ],
-        compiler_params=pltpu.CompilerParams(vmem_limit_bytes=48 << 20),
+        compiler_params=pltpu.CompilerParams(vmem_limit_bytes=60 * 1024 * 1024),
         name="positions",
-    )(mine, others, tile, halo, probe, amp_own, amp_got, table)
+    )(*own, *got, tile, halo, probe, amp_own, amp_got, table)
 
 
 class Place:
@@ -255,8 +274,13 @@
     pl.semaphore_wait(barrier, len(devices))
 
 
-def sums_kernel(sizes, grad, prb, upd_out, prb_out,
-                near, quarter, near2, slim, shifted,
+def cube(index):
+    high, odd = index // 2, lax.rem(index, 2)
+    return ((lax.rem(high + odd, 2), index + 1 - 2 * odd), (high, 3 - index))
+
+
+def sums_kernel(sizes, object_scale, probe_scaling, grad, prb, upd_out, prb_out,
+                near1, kept1, near2, kept2, near3, kept3, near4, kept4, shifted,
                 give, got, mixed, first, held, second, small, third,
                 send, recv):
     at = Place(sizes)
@@ -278,15 +302,62 @@
           + [at.along_y(d)[1] for d in range(1, at.ny)]
           + [at.along_x(d)[1] for d in range(1, at.nx)])
 
-    height, width = grad.shape[1], grad.shape[2]
-    xrows = height // at.nx
-    hrows = xrows // at.nhi
+    height = grad.shape[1]
     total = prb.shape[0]
     half = total // 2
     quart = half // 2
 
-    def block(index, rows):
-        return pl.ds(pl.multiple_of(index * rows, 8), rows)
+    bits = []
+    for h in range(2):
+        xb = [(b, at.device(at.z, at.y, at.core, to)) for b, to in cube(at.x)]
+        yb = [(b, at.device(at.z, to * at.nlo + at.lo, at.core, at.x)) for b, to in cube(at.hi)]
+        bits.append((xb if h == 0 else xb[::-1]) + (yb if h == 0 else yb[::-1]))
+    cut = [height // 4, height // 8, height // 16, height // 32]
+    near = [near1, near2, near3, near4]
+    kept = [kept1, kept2, kept3, kept4]
+
+    def object_source(h, stage):
+        if stage == 0:
+            return grad, h * (height // 2)
+        return kept[stage - 1].at[h], 0
+
+    def object_send(stage):
+        out = []
+        for h in range(2):
+            bit, device = bits[h][stage]
+            src, base = object_source(h, stage)
+            rows = pl.ds(pl.multiple_of(base + (1 - bit) * cut[stage], 8), cut[stage])
+            out.append(copy(src.at[:, rows, :], near[stage].at[h], device))
+        return out
+
+    def object_add(stage, copies):
+        for h in range(2):
+            copies[h].wait_recv()
+            bit, _ = bits[h][stage]
+            src, base = object_source(h, stage)
+            mine = base + bit * cut[stage]
+
+            def add(r, h=h, src=src, mine=mine):
+                rows = pl.ds(r, 24)
+                for k in range(2):
+                    kept[stage][h, k, rows, :] = (
+                        src[k, pl.ds(pl.multiple_of(mine + r, 8), 24), :] + near[stage][h, k, rows, :])
+            rows_loop(cut[stage], 24, add)
+
+    def object_place(h, stages):
+        base = h * (height // 2)
+        for stage in range(stages):
+            base += bits[h][stage][0] * cut[stage]
+        return base
+
+    def object_gather(stage):
+        out = []
+        for h in range(2):
+            rows = pl.ds(pl.multiple_of(object_place(h, stage + 1), 8), cut[stage])
+            out.append(copy(upd_out.at[rows, :], upd_out.at[rows, :], bits[h][stage][1]))
+        return out
+
+    o = object_send(0)
 
     other_base = (1 - at.core) * half
     my_base = at.core * half
@@ -295,12 +366,6 @@
         give[pl.ds(r, 32), :] = prb[pl.ds(pl.multiple_of(other_base + r, 8), 32), :].astype(BF16)
     rows_loop(half, 32, cast_half)
     p0 = copy(give, got, at.partner())
-
-    o1 = []
-    for d in range(1, at.nx):
-        to, device = at.along_x(d)
-        o1.append(copy(grad.at[:, block(to, xrows), :], near.at[d - 1], device))
-
     p0.wait_recv()
 
     def mix(r):
@@ -311,14 +376,20 @@
 
     axes = ((at.along_z, at.along_y, at.nz, at.ny, at.z, at.y),
             (at.along_y, at.along_z, at.ny, at.nz, at.y, at.z))
+
+    def far_first(n):
+        return sorted(range(1, n), key=lambda d: (-min(d, n - d), d))
+
     p1 = [[], []]
-    for d in range(1, max(at.nz, at.ny)):
-        for h, (one, _, n1, n2, c1, c2) in enumerate(axes):
-            if d < n1:
-                to, device = one(d)
-                rows = quart // n1
-                src = mixed.at[pl.ds(pl.multiple_of(h * quart + to * rows, 16), rows), :]
-                p1[h].append(copy(src, first.at[h, d - 1, pl.ds(0, rows), :], device))
+    for h, (one, _, n1, n2, c1, c2) in enumerate(axes):
+        for d in far_first(n1):
+            to, device = one(d)
+            rows = quart // n1
+            src = mixed.at[pl.ds(pl.multiple_of(h * quart + to * rows, 16), rows), :]
+            p1[h].append(copy(src, first.at[h, d - 1, pl.ds(0, rows), :], device))
+
+    object_add(0, o)
+    o = object_send(1)
 
     p2 = [[], []]
     for h, (_, two, n1, n2, c1, c2) in enumerate(axes):
@@ -335,40 +406,24 @@
             held[h, pl.ds(r, 16), :] = acc
         rows_loop(rows, 16, add_first)
         sub = rows // n2
-        for d in range(1, n2):
+        for d in far_first(n2):
             to, device = two(d)
-            p2[h].append(copy(held.at[h, block(to, sub), :], second.at[h, d - 1], device))
-
-    for c in o1:
-        c.wait_recv()
-    xbase = at.x * xrows
-
-    def add_near(r):
-        rows = pl.ds(r, 8)
-        for k in range(2):
-            acc = grad[k, pl.ds(pl.multiple_of(xbase + r, 8), 8), :]
-            for d in range(at.nx - 1):
-                acc += near[d, k, rows, :]
-            quarter[k, rows, :] = acc
-    rows_loop(xrows, 8, add_near)
-    o2 = []
-    for d in range(1, at.nhi):
-        to, device = at.along_hi(d)
-        o2.append(copy(quarter.at[:, block(to, hrows), :], near2.at[d - 1], device))
+            src = held.at[h, pl.ds(pl.multiple_of(to * sub, 8), sub), :]
+            p2[h].append(copy(src, second.at[h, d - 1], device))
+
+    object_add(1, o)
+    o = object_send(2)
 
     sub = quart // (at.nz * at.ny)
     for h, (_, _, n1, n2, c1, c2) in enumerate(axes):
         for c in p2[h]:
             c.wait_recv()
-        acc = held[h, block(c2, sub), :]
+        acc = held[h, pl.ds(pl.multiple_of(c2 * sub, 8), sub), :]
         for d in range(n2 - 1):
             acc += second[h, d]
         small[h] = acc
         third[at.x, h] = acc
-    p3 = []
-    for d in range(1, at.nx):
-        _, device = at.along_x(d)
-        p3.append(copy(small, third.at[at.x], device))
+    p3 = [copy(small, third.at[at.x], at.along_x(d)[1]) for d in far_first(at.nx)]
     for c in p3:
         c.wait_recv()
     p4 = [[], []]
@@ -377,63 +432,93 @@
         for k in range(1, at.nx):
             acc += third[k, h]
         rows = pl.ds(pl.multiple_of(my_base + h * quart + c1 * (quart // n1) + c2 * sub, 8), sub)
-        prb_out[rows, :] = acc
-        for d in range(1, n2):
+        prb_out[rows, :] = probe_scaling * acc
+        for d in far_first(n2):
             p4[h].append(copy(prb_out.at[rows, :], prb_out.at[rows, :], two(d)[1]))
 
-    for c in o2:
-        c.wait_recv()
-    hbase = at.hi * hrows
-
-    def add_near2(r):
-        rows = pl.ds(r, 8)
-        for k in (1, 0):
-            acc = quarter[k, pl.ds(pl.multiple_of(hbase + r, 8), 8), :]
-            for d in range(at.nhi - 1):
-                acc += near2[d, k, rows, :]
-            slim[k, rows, :] = acc
-    rows_loop(hrows, 8, add_near2)
-    o0 = copy(slim.at[1], shifted, at.tile(1))
-
-    p5 = [[], []]
-    for h, (one, _, n1, n2, c1, c2) in enumerate(axes):
+    object_add(2, o)
+    o = object_send(3)
+
+    def share(h, origin, device, part=None):
+        n1 = axes[h][2]
+        size = quart // n1
+        base = my_base + h * quart + lax.rem(origin + n1, n1) * size
+        if part is not None:
+            size = size // 2
+            base += part * size
+        rows = pl.ds(pl.multiple_of(base, 8), size)
+        return copy(prb_out.at[rows, :], prb_out.at[rows, :], device)
+
+    p6 = []
+    steps = max(at.nz, at.ny) // 2
+
+    def ring_send(k):
+        out = {}
+        for h, (one, _, n1, _, c1, _) in enumerate(axes):
+            if 2 * k > n1:
+                continue
+            for side in range(2):
+                ahead = one(1 if side == 0 else n1 - 1)[1]
+                origin = c1 - (k - 1) if side == 0 else c1 + (k - 1)
+                out[h, side] = share(h, origin, ahead, side if 2 * k == n1 else None)
+        return out
+
+    def ring_wait(k, sent):
+        for h, (one, _, n1, _, c1, _) in enumerate(axes):
+            if 2 * k > n1:
+                continue
+            for side in range(2):
+                sent[h, side].wait_recv()
+
+    def ring_share(k):
+        for h, (_, _, n1, _, c1, _) in enumerate(axes):
+            if 2 * k > n1:
+                continue
+            p6.append(share(h, c1 - k, at.partner()))
+            if 2 * k < n1:
+                p6.append(share(h, c1 + k, at.partner()))
+
+    for h in range(2):
         for c in p4[h]:
             c.wait_recv()
-        rows = pl.ds(pl.multiple_of(my_base + h * quart + c1 * (quart // n1), 8), quart // n1)
-        for d in range(1, n1):
-            p5[h].append(copy(prb_out.at[rows, :], prb_out.at[rows, :], one(d)[1]))
-
-    o0.wait_recv()
-    obase = xbase + hbase
-
-    def finish(r):
-        upd_out[pl.ds(pl.multiple_of(obase + r, 8), 8), :] = slim[0, pl.ds(r, 8), :] + shifted[pl.ds(r, 8), :]
-    rows_loop(hrows, 8, finish)
-    o3 = []
-    orow = pl.ds(pl.multiple_of(obase, 8), hrows)
-    for d in range(1, at.nhi):
-        o3.append(copy(upd_out.at[orow, :], upd_out.at[orow, :], at.along_hi(d)[1]))
-
-    p6 = []
-    for h, (one, _, n1, n2, c1, c2) in enumerate(axes):
-        rows = pl.ds(pl.multiple_of(my_base + h * quart + c1 * (quart // n1), 8), quart // n1)
-        p6.append(copy(prb_out.at[rows, :], prb_out.at[rows, :], at.partner()))
-
-    for c in o3:
+    ring = ring_send(1)
+    for h in range(2):
+        p6.append(share(h, axes[h][4], at.partner()))
+
+    object_add(3, o)
+    o = copy(kept4.at[:, 1], shifted, at.tile(1))
+
+    def ring_step(k, ring):
+        if k > steps:
+            return None
+        ring_wait(k, ring)
+        after = ring_send(k + 1) if k < steps else None
+        ring_share(k)
+        return after
+
+    ring = ring_step(1, ring)
+    o.wait_recv()
+    for h in range(2):
+        place = object_place(h, 4)
+
+        def finish(r, h=h, place=place):
+            rows = pl.ds(r, 8)
+            upd_out[pl.ds(pl.multiple_of(place + r, 8), 8), :] = object_scale * (kept4[h, 0, rows, :] + shifted[h, rows, :])
+        rows_loop(cut[3], 8, finish)
+    o = object_gather(3)
+    ring = ring_step(2, ring)
+    for c in o:
         c.wait_recv()
-    o4 = []
-    xrow = pl.ds(pl.multiple_of(xbase, 8), xrows)
-    for d in range(1, at.nx):
-        o4.append(copy(upd_out.at[xrow, :], upd_out.at[xrow, :], at.along_x(d)[1]))
-
-    for d in range(1, max(at.nz, at.ny)):
-        for h, (_, _, n1, n2, c1, c2) in enumerate(axes):
-            if d < n1:
-                p5[h][d - 1].wait_recv()
-                origin = lax.rem(c1 + n1 - d, n1)
-                rows = pl.ds(pl.multiple_of(my_base + h * quart + origin * (quart // n1), 8), quart // n1)
-                p6.append(copy(prb_out.at[rows, :], prb_out.at[rows, :], at.partner()))
-    for c in o4:
+    o = object_gather(2)
+    ring = ring_step(3, ring)
+    for c in o:
+        c.wait_recv()
+    o = object_gather(1)
+    ring = ring_step(4, ring)
+    for c in o:
+        c.wait_recv()
+    o = object_gather(0)
+    for c in o:
         c.wait_recv()
     for c in p6:
         c.wait_recv()
@@ -441,55 +526,46 @@
         c.wait_send()
 
 
-def count_copies(sizes):
-    nz, nlo, nc, nx, nhi = sizes
-    ny = nlo * nhi
-    return 2 + 2 * (nx - 1) + 2 * (nhi - 1) + 4 * (nz - 1 + ny - 1) + (nx - 1) + (nz + ny)
-
-
-def sums(sizes, grad, prb):
+def sums(sizes, grad, prb, object_scale=1.0, probe_scaling=1.0):
     nz, nlo, nc, nx, nhi = sizes
     ny = nlo * nhi
     height, width = grad.shape[1:]
     total, pw = prb.shape
-    xrows, hrows = height // nx, height // nx // nhi
     half, quart = total // 2, total // 4
-    n1, small_n = max(nz, ny), min(nz, ny)
+    long, short = max(nz, ny), min(nz, ny)
     sub = quart // (nz * ny)
     vmem = pl.BlockSpec(memory_space=pltpu.VMEM)
-    copies = count_copies(sizes)
+    stages = []
+    for k in (4, 8, 16, 32):
+        stages += [pltpu.VMEM((2, 2, height // k, width), F32)] * 2
     return pl.pallas_call(
-        functools.partial(sums_kernel, sizes),
+        functools.partial(sums_kernel, sizes, object_scale, probe_scaling),
         out_shape=(jax.ShapeDtypeStruct((height, width), F32), jax.ShapeDtypeStruct((total, pw), F32)),
         in_specs=[vmem, vmem],
         out_specs=(vmem, vmem),
-        scratch_shapes=[
-            pltpu.VMEM((nx - 1, 2, xrows, width), F32),
-            pltpu.VMEM((2, xrows, width), F32),
-            pltpu.VMEM((nhi - 1, 2, hrows, width), F32),
-            pltpu.VMEM((2, hrows, width), F32),
-            pltpu.VMEM((hrows, width), F32),
+        scratch_shapes=stages + [
+            pltpu.VMEM((2, height // 32, width), F32),
             pltpu.VMEM((half, pw), BF16),
             pltpu.VMEM((half, pw), BF16),
             pltpu.VMEM((half, pw), BF16),
-            pltpu.VMEM((2, n1 - 1, quart // small_n, pw), BF16),
-            pltpu.VMEM((2, quart // small_n, pw), F32),
-            pltpu.VMEM((2, n1 - 1, sub, pw), F32),
+            pltpu.VMEM((2, long - 1, quart // short, pw), BF16),
+            pltpu.VMEM((2, quart // short, pw), F32),
+            pltpu.VMEM((2, long - 1, sub, pw), F32),
             pltpu.VMEM((2, sub, pw), F32),
             pltpu.VMEM((nx, 2, sub, pw), F32),
-            pltpu.SemaphoreType.DMA((copies,)),
-            pltpu.SemaphoreType.DMA((copies,)),
+            pltpu.SemaphoreType.DMA((COPIES,)),
+            pltpu.SemaphoreType.DMA((COPIES,)),
         ],
         compiler_params=pltpu.CompilerParams(
-            collective_id=1, has_side_effects=True, vmem_limit_bytes=48 << 20),
+            collective_id=1, has_side_effects=True, vmem_limit_bytes=60 * 1024 * 1024),
         name="sums",
     )(grad, prb)
 
 
-def spread_kernel(sizes, tile, amp, meta, halo, amp_got, meta_got, send, recv):
+def spread_kernel(sizes, tile, amp, rows, cols, count, halo, amp_got, rows_got, cols_got, count_got, send, recv):
     at = Place(sizes)
-    keep = amp.shape[0] - amp_got.shape[0]
     moved = amp_got.shape[0]
+    keep = amp.shape[0] - moved
     devices = [at.along_x(d)[1] for d in range(1, moved + 1)]
     greet([at.tile(1), at.tile(-1)] + devices)
     copies = []
@@ -504,50 +580,46 @@
 
     copy(tile, halo, at.tile(-1))
     for k, device in enumerate(devices):
-        copy(meta, meta_got.at[k], device)
         copy(amp.at[keep + k], amp_got.at[k], device)
+        copy(rows, rows_got.at[k], device)
+        copy(cols, cols_got.at[k], device)
+        copy(count, count_got.at[k], device)
     for c in copies:
         c.wait()
 
 
-def spread(sizes, tile, amp, meta, moved):
+def spread(sizes, moved, tile, amp, *meta):
     anywhere = pl.BlockSpec(memory_space=pl.ANY)
+    copies = 1 + (1 + len(meta)) * moved
     return pl.pallas_call(
         functools.partial(spread_kernel, sizes),
         out_shape=(
             jax.ShapeDtypeStruct(tile.shape, tile.dtype),
             jax.ShapeDtypeStruct((moved,) + amp.shape[1:], amp.dtype),
-            jax.ShapeDtypeStruct((moved,) + meta.shape, meta.dtype),
-        ),
-        in_specs=[anywhere] * 3,
-        out_specs=(anywhere,) * 3,
-        scratch_shapes=[pltpu.SemaphoreType.DMA((1 + 2 * moved,))] * 2,
-        compiler_params=pltpu.CompilerParams(collective_id=0, has_side_effects=True),
+        ) + tuple(jax.ShapeDtypeStruct((moved,) + m.shape, m.dtype) for m in meta),
+        in_specs=[pl.BlockSpec(memory_space=pltpu.HBM)] * (2 + len(meta)),
+        out_specs=(anywhere,) * (2 + len(meta)),
+        scratch_shapes=[pltpu.SemaphoreType.DMA((copies,))] * 2,
+        compiler_params=pltpu.CompilerParams(
+            collective_id=0, has_side_effects=True, vmem_limit_bytes=60 * 1024 * 1024),
         name="spread",
-    )(tile, amp, meta)
+    )(tile, amp, *meta)
 
 
 def on_device(object_tiles, probe_modes, amplitudes, row_offsets, col_offsets, slot_counts):
     slots = amplitudes.shape[2]
-    edge = (lax.axis_index("tile") == lax.axis_size("tile") - 1).astype(jnp.int32)
-    pad = ((0, 0), (0, 128 - slots))
-    meta = jnp.concatenate([
-        jnp.pad(row_offsets[0], pad),
-        jnp.pad(col_offsets[0], pad),
-        jnp.full((1, 128), slot_counts[0, 0]),
-        jnp.full((1, 128), edge),
-        jnp.zeros((4, 128), jnp.int32),
-    ])
-    halo, amp_got, meta_got = spread(SIZES, object_tiles, amplitudes[0, 0], meta, slots - KEEP)
+    meta = (row_offsets[0], col_offsets[0], slot_counts)
+    halo, amp_got, *meta_got = spread(SIZES, slots - KEEP, object_tiles, amplitudes[0, 0], *meta)
     grad, probe_grad = positions(
         meta, meta_got, object_tiles, halo, probe_modes, amplitudes[0, 0], amp_got,
         dft_tables(probe_modes.shape[2]),
     )
     width = object_tiles.shape[2]
-    update, summed = sums(SIZES, grad.reshape(2, -1, width), probe_grad.reshape(-1, probe_modes.shape[3]))
-    new_object = object_tiles + object_step * update.reshape(object_tiles.shape)
     factor = probe_scale / math.sqrt(lax.axis_size("tile") * lax.axis_size("scan"))
-    new_probe = probe_modes.astype(F32) + factor * summed.reshape(probe_modes.shape)
+    update, change = sums(
+        SIZES, grad.reshape(2, -1, width), probe_grad.reshape(-1, probe_modes.shape[3]), object_step, factor)
+    new_object = object_tiles + update.reshape(object_tiles.shape)
+    new_probe = probe_modes.astype(F32) + change.reshape(probe_modes.shape)
     return (new_object, new_probe)
 
 

time: 126 us -> 115 us (0.913)
  the two profiles are of different devices: /device:TPU:1 before, /device:TPU:2 now
where the time goes in v2:
time: 115 us; the launch traced here: 114 us
  Pallas kernels  108 us (94%)
  other arithmetic  5.4 us (5%)
  between operations  1.32 us (1%)
    pallas_call x1, Pallas kernels, sums(): pl.pallas_call(functools.partial(sums_kernel, sizes, object_scale, probe_...  62.7 us
    pallas_call x1, Pallas kernels, positions(): pl.pallas_call(positions_kernel, out_shape=(jax.ShapeDtypeStruct((2, 2, h...  24.6 us
    pallas_call x1, Pallas kernels, spread(): pl.pallas_call(functools.partial(spread_kernel, sizes), out_shape=(jax.Sh...  20.3 us
    add x1, other arithmetic, on_device(): new_probe = probe_modes.astype(F32) + change.reshape(probe_modes.shape)  3.2 us

profile of v2, /device:TPU:2, one launch (start us, length us, event | category | flops | bytes accessed | tf_op | source)
XLA Modules:
  0.0 114.3 jit_solution(2757784101447127348)
XLA Ops:
  1.3 20.3 %spread.1 = (f32[2,384,256]{2,1,0:T(8,128)}, bf16[3,256,256]{2,1,0:T(8,128)(2,1)}, s32[3,1,5]{2,1,0:T(1,128)}, s32[3,1,5]{2,1,0:T(1,128)}, s32[3,1,1]{2,1,0:T(1,128)}) custom-call(f32[2,384,256]{2,1,0:T(8,128)} %tile_in.1, bf16[5,256,256]{2,1,0:T(8,128)(2,1)} %bitcast.7, s32[1,5]{1,0:T(1,128)} %bitcast.13, s32[1,5]{1,0:T(1,128)} %bitcast.15, ...), custom_call_target="tpu_custom_call" | custom-call | tf_op jit(solution)/shard_map/spread/pallas_call | solution.py:594
  21.6 24.6 %positions.1 = (f32[2,2,384,256]{3,2,1,0:T(8,128)}, f32[2,4,256,256]{3,2,1,0:T(8,128)}) custom-call(s32[1,5]{1,0:T(1,128)} %bitcast.14, s32[1,5]{1,0:T(1,128)} %bitcast.16, s32[1,1]{1,0:T(1,128)S(6)} %copy.9.count.count_own_in, s32[3,1,5]{2,1,0:T(1,128)} %get-tuple-element.11.rows_got_in, s32[3,1,5]{2,1,0:T(1,128)} %get-tuple-element.12.cols_got_in, ...), custom_call_target="tpu_custom_call" | custom-call | tf_op jit(solution)/shard_map/positions/pallas_call | solution.py:202
  46.2 0.0 copy-start
  46.2 62.7 %sums.1 = (f32[768,256]{1,0:T(8,128)}, f32[2048,256]{1,0:T(8,128)}) custom-call(f32[2,768,256]{2,1,0:T(8,128)} %bitcast.11, f32[2048,256]{1,0:T(8,128)} %bitcast.9), custom_call_target="tpu_custom_call" | custom-call | tf_op jit(solution)/shard_map/sums/pallas_call | solution.py:541
  108.9 0.0 copy-start.1
  108.9 0.0 copy-done
  108.9 2.2 %add.6 = f32[2,384,256]{2,1,0:T(8,128)} add(f32[2,384,256]{2,1,0:T(8,128)S(1)} %copy-done, f32[2,384,256]{2,1,0:T(8,128)} %bitcast.12) | non-fusion elementwise | flops 196608 | bytes 2359296 | tf_op jit(solution)/shard_map/add | solution.py:621
  111.1 0.0 copy-done.1
  111.1 3.2 %convert_add_fusion = f32[2,4,256,256]{3,2,1,0:T(8,128)} fusion(f32[2,4,256,256]{3,2,1,0:T(8,128)} %bitcast.10, bf16[2,4,256,256]{3,2,1,0:T(8,128)(2,1)S(1)} %copy-done.1), kind=kLoop, calls=%fused_computation | loop fusion | flops 1048576 | bytes 5242880 | tf_op jit(solution)/shard_map/add | solution.py:622
Async XLA Ops:
  46.2 62.8 %copy-start = (f32[2,384,256]{2,1,0:T(8,128)S(1)}, f32[2,384,256]{2,1,0:T(8,128)}, u32[]{:S(2)}) copy-start(f32[2,384,256]{2,1,0:T(8,128)} %tile_in.1) | copy-start | bytes 2359300
  108.9 2.2 %copy-start.1 = (bf16[2,4,256,256]{3,2,1,0:T(8,128)(2,1)S(1)}, bf16[2,4,256,256]{3,2,1,0:T(8,128)(2,1)}, u32[]{:S(2)}) copy-start(bf16[2,4,256,256]{3,2,1,0:T(8,128)(2,1)} %probe_in.1) | copy-start | bytes 3145732

commit v3 on v2

v3 whole, which is shorter than its diff:
```python
import functools
import math

import jax
import jax.numpy as jnp
import numpy as np
from jax import lax
from jax.experimental import pallas as pl
from jax.experimental.pallas import tpu as pltpu
from jax.sharding import PartitionSpec as P

F32, BF16 = jnp.float32, jnp.bfloat16
MESH = pl.DeviceIdType.MESH
KEEP = 2
COPIES = 136
ORDER = "rlpprlprlprlrlplrplpplpplpplpplpllpppppppllllllllll"
SIZES = (8, 2, 2, 4, 4)
object_step = 0.1
probe_scale = 0.5


def dft_tables(extent):
    index = np.arange(extent)
    angle = (index[:, None] * index[None, :] % extent) * (2.0 * math.pi / extent)
    factor = 1.0 / math.sqrt(extent)
    table = np.stack([np.cos(angle) * factor, -np.sin(angle) * factor])
    return jnp.asarray(table.astype(np.float32)).astype(BF16)


def rows_loop(total, step, body, unroll=1):
    def trip(i, carry):
        body(pl.multiple_of(i * step, step))
        return carry
    lax.fori_loop(0, total // step, trip, 0, unroll=unroll)


def dot(a, b):
    return jnp.dot(a, b, preferred_element_type=F32)


def positions_kernel(rows_own_in, cols_own_in, count_own_in, rows_got_in, cols_got_in, count_got_in,
                     tile_in, halo_in, probe_in, amp_own, amp_got, table_in,
                     grad_out, prb_out,
                     rows_own, cols_own, count_own, rows_got, cols_got, count_got, ext, probe, table,
                     amp, patch, stack, side, wide, term, forward, inverse, arrived, loaded):
    n = probe.shape[2]
    modes = probe.shape[1]
    blocks, _, height, lane = grad_out.shape
    near, inner = blocks // 2, n // lane
    moves = [(tile_in.at[:, :, pl.ds(b * lane, lane)], ext.at[b]) for b in range(near)]
    moves += [(halo_in.at[:, :, pl.ds(b * lane, lane)], ext.at[near + b]) for b in range(near)]
    moves += [
        (probe_in, probe), (table_in, table),
        (rows_own_in, rows_own), (cols_own_in, cols_own), (count_own_in, count_own),
        (rows_got_in, rows_got), (cols_got_in, cols_got), (count_got_in, count_got),
    ]
    loads = [pltpu.make_async_copy(src, dst, loaded.at[k]) for k, (src, dst) in enumerate(moves)]
    for load in loads:
        load.start()
    edge = lax.axis_index("tile") == lax.axis_size("tile") - 1

    def clear(at):
        grad_out[:, :, pl.ds(at, 16), :] = jnp.zeros((blocks, 2, 16, lane), F32)
    rows_loop(height, 16, clear)

    def clear_probe(at):
        prb_out[:, :, pl.ds(at, 16), :] = jnp.zeros((2, modes, 16, n), F32)
    rows_loop(n, 16, clear_probe)
    term[:, :8, :] = jnp.zeros((2, 8, n), F32)
    term[:, n + 8:, :] = jnp.zeros((2, 8, n), F32)
    for load in loads:
        load.wait()

    @pl.when(edge)
    def _():
        def drop(at):
            ext[near:, :, pl.ds(at, 16), :] = jnp.zeros((blocks - near, 2, 16, lane), F32)
        rows_loop(height, 16, drop)
    forward[:n, :n] = table[0]
    forward[n:, n:] = table[0]
    forward[n:, :n] = table[1]
    forward[:n, n:] = -table[1]
    inverse[:n, :n] = table[0]
    inverse[n:, n:] = table[0]
    inverse[n:, :n] = -table[1]
    inverse[:n, n:] = table[1]

    def position(r, c):
        base = pl.multiple_of(jnp.minimum(r // 8 * 8, height - n - 8), 8)
        down = r - base
        block, right = c // lane, lax.rem(c, lane)
        up, left = lax.rem(8 - down, 8), lax.rem(lane - right, lane)
        lanes = lax.broadcasted_iota(jnp.int32, (8, lane), 1)
        rows8 = lax.broadcasted_iota(jnp.int32, (8, lane), 0)
        in_lanes, in_rows = lanes < lane - right, rows8 < 8 - down
        out_lanes, out_rows = lanes >= right, rows8 >= down

        def cut(at):
            for p in range(2):
                turned = [
                    pltpu.roll(ext[block + j, p, pl.ds(pl.multiple_of(base + at, 8), 40), :], left, 1).reshape(5, 8, lane)
                    for j in range(inner + 1)
                ]
                for j in range(inner):
                    x = jnp.where(in_lanes, turned[j], turned[j + 1])
                    x = pltpu.roll(x, up, 1)
                    x = jnp.where(in_rows, x[:4], x[1:])
                    patch[p, pl.ds(at, 32), j * lane:(j + 1) * lane] = x.reshape(32, lane)
        rows_loop(n, 32, cut, unroll=True)

        def make_psi(at):
            rows, low = pl.ds(at, 16), pl.ds(pl.multiple_of(at + n, 16), 16)
            xr, xi = patch[0, rows, :], patch[1, rows, :]
            for m in range(modes):
                pr = probe[0, m, rows, :].astype(F32)
                pi = probe[1, m, rows, :].astype(F32)
                stack[m, rows, :] = (pr * xr - pi * xi).astype(BF16)
                stack[m, low, :] = (pr * xi + pi * xr).astype(BF16)
        rows_loop(n, 16, make_psi, unroll=True)

        for m in range(modes):
            a = dot(forward[...], stack[m]).astype(BF16)
            side[m, :, :n] = a[:n]
            side[m, :, n:] = a[n:]
        for m in range(modes):
            wide[m] = dot(side[m], inverse[...])

        pltpu.make_async_copy(amp_own.at[0], amp, arrived).wait()

        def make_d(at):
            rows, low = pl.ds(at, 16), pl.ds(pl.multiple_of(at + n, 16), 16)
            total = jnp.zeros((16, n), F32)
            for m in range(modes):
                fr, fi = wide[m, rows, :n], wide[m, rows, n:]
                total += fr * fr + fi * fi
            factor = amp[rows, :].astype(F32) / jnp.sqrt(total + 1.0) - 1.0
            for m in range(modes):
                stack[m, rows, :] = (wide[m, rows, :n] * factor).astype(BF16)
                stack[m, low, :] = (wide[m, rows, n:] * factor).astype(BF16)
        rows_loop(n, 16, make_d, unroll=True)

        for m in range(modes):
            b = dot(inverse[...], stack[m]).astype(BF16)
            side[m, :, :n] = b[:n]
            side[m, :, n:] = b[n:]
        for m in range(modes):
            wide[m] = dot(side[m], forward[...])

        def finish(at):
            rows = pl.ds(at, 16)
            xr, xi = patch[0, rows, :], patch[1, rows, :]
            tr = jnp.zeros((16, n), F32)
            ti = jnp.zeros((16, n), F32)
            for m in range(modes):
                er, ei = wide[m, rows, :n], wide[m, rows, n:]
                pr = probe[0, m, rows, :].astype(F32)
                pi = probe[1, m, rows, :].astype(F32)
                tr += pr * er + pi * ei
                ti += pr * ei - pi * er
                prb_out[0, m, rows, :] += xr * er + xi * ei
                prb_out[1, m, rows, :] += xr * ei - xi * er
            below = pl.ds(pl.multiple_of(at + 8, 8), 16)
            term[0, below, :] = tr
            term[1, below, :] = ti
        rows_loop(n, 16, finish, unroll=True)

        def paste(at):
            rows = pl.ds(pl.multiple_of(base + at, 8), 24)
            for p in range(2):
                turned = []
                for j in range(inner):
                    x = term[p, pl.ds(at, 32), j * lane:(j + 1) * lane].reshape(4, 8, lane)
                    x = pltpu.roll(x, lax.rem(down, 8), 1)
                    x = jnp.where(out_rows, x[1:], x[:3]).reshape(24, lane)
                    turned.append(pltpu.roll(x, right, 1).reshape(3, 8, lane))
                for j in range(inner + 1):
                    low = turned[j] if j < inner else jnp.zeros((3, 8, lane), F32)
                    high = turned[j - 1] if j > 0 else jnp.zeros((3, 8, lane), F32)
                    grad_out[block + j, p, rows, :] += jnp.where(out_lanes, low, high).reshape(24, lane)
        rows_loop(n + 8, 24, paste, unroll=True)

    slots = KEEP + amp_got.shape[0]

    def item_trip(item, carry):
        own = item < KEEP
        other = jnp.maximum(item - KEEP, 0)
        r = jnp.where(own, rows_own[0, item], rows_got[other, 0, item])
        c = jnp.where(own, cols_own[0, item], cols_got[other, 0, item])
        count = jnp.where(own, count_own[0, 0], count_got[other, 0, 0])

        @pl.when(item < count)
        def _():
            @pl.when(own)
            def _():
                pltpu.make_async_copy(amp_own.at[item], amp, arrived).start()

            @pl.when(jnp.logical_not(own))
            def _():
                pltpu.make_async_copy(amp_got.at[other], amp, arrived).start()
            position(r, c)
        return carry
    lax.fori_loop(0, slots, item_trip, 0)

    @pl.when(edge)
    def _():
        def drop(at):
            grad_out[near:, :, pl.ds(at, 16), :] = jnp.zeros((blocks - near, 2, 16, lane), F32)
        rows_loop(height, 16, drop)


def positions(own, got, tile, halo, probe, amp_own, amp_got, table):
    _, modes, n, _ = probe.shape
    height, tw = tile.shape[1:]
    vmem, anywhere = pl.BlockSpec(memory_space=pltpu.VMEM), pl.BlockSpec(memory_space=pl.ANY)
    hbm = pl.BlockSpec(memory_space=pltpu.HBM)
    return pl.pallas_call(
        positions_kernel,
        out_shape=(
            jax.ShapeDtypeStruct((2 * tw // 128, 2, height, 128), F32),
            jax.ShapeDtypeStruct((2, modes, n, n), F32),
        ),
        in_specs=[hbm] * 3 + [anywhere] * 3 + [hbm, anywhere, hbm, hbm, anywhere, hbm],
        out_specs=(vmem, vmem),
        scratch_shapes=[pltpu.SMEM(m.shape, m.dtype) for m in (*own, *got)] + [
            pltpu.VMEM((2 * tw // 128, 2, height, 128), F32),
            pltpu.VMEM(probe.shape, BF16),
            pltpu.VMEM(table.shape, BF16),
            pltpu.VMEM((n, n), BF16),
            pltpu.VMEM((2, n, n), F32),
            pltpu.VMEM((modes, 2 * n, n), BF16),
            pltpu.VMEM((modes, n, 2 * n), BF16),
            pltpu.VMEM((modes, n, 2 * n), F32),
            pltpu.VMEM((2, n + 16, n), F32),
            pltpu.VMEM((2 * n, 2 * n), BF16),
            pltpu.VMEM((2 * n, 2 * n), BF16),
            pltpu.SemaphoreType.DMA,
            pltpu.SemaphoreType.DMA((8 + 2 * tw // 128,)),
        ],
        compiler_params=pltpu.CompilerParams(vmem_limit_bytes=60 * 1024 * 1024),
        name="positions",
    )(*own, *got, tile, halo, probe, amp_own, amp_got, table)


class Place:
    def __init__(self, sizes):
        self.nz, self.nlo, self.nc, self.nx, self.nhi = sizes
        self.ny = self.nlo * self.nhi
        self.tiles, self.scans = self.nz * self.nlo * self.nc, self.nx * self.nhi
        self.t, self.s = lax.axis_index("tile"), lax.axis_index("scan")
        self.core = lax.rem(self.t, self.nc)
        self.lo = lax.rem(self.t // self.nc, self.nlo)
        self.z = self.t // (self.nc * self.nlo)
        self.x, self.hi = self.s // self.nhi, lax.rem(self.s, self.nhi)
        self.y = self.hi * self.nlo + self.lo

    def device(self, z, y, core, x):
        lo, hi = lax.rem(y, self.nlo), y // self.nlo
        return {"tile": (z * self.nlo + lo) * self.nc + core, "scan": x * self.nhi + hi}

    def along_z(self, d):
        at = lax.rem(self.z + d, self.nz)
        return at, self.device(at, self.y, self.core, self.x)

    def along_y(self, d):
        at = lax.rem(self.y + d, self.ny)
        return at, self.device(self.z, at, self.core, self.x)

    def along_hi(self, d):
        at = lax.rem(self.hi + d, self.nhi)
        return at, self.device(self.z, at * self.nlo + self.lo, self.core, self.x)

    def along_x(self, d):
        at = lax.rem(self.x + d, self.nx)
        return at, self.device(self.z, self.y, self.core, at)

    def tile(self, d):
        return {"tile": lax.rem(self.t + self.tiles + d, self.tiles), "scan": self.s}

    def partner(self):
        return self.device(self.z, self.y, 1 - self.core, self.x)


def greet(devices):
    barrier = pltpu.get_barrier_semaphore()
    for device in devices:
        pl.semaphore_signal(barrier, inc=1, device_id=device, device_id_type=MESH)
    pl.semaphore_wait(barrier, len(devices))


def cube(index):
    high, odd = index // 2, lax.rem(index, 2)
    return ((lax.rem(high + odd, 2), index + 1 - 2 * odd), (high, 3 - index))


def sums_kernel(sizes, object_scale, probe_scaling, grad, prb, upd_low, upd_high, prb_out,
                near1, kept1, near2, kept2, near3, kept3, near4, kept4, shifted,
                give, got, mixed, first, held, second, small, third,
                send, recv):
    at = Place(sizes)
    used = [0]
    started = []

    def copy(src, dst, device):
        k = used[0]
        used[0] += 1
        c = pltpu.make_async_remote_copy(
            src_ref=src, dst_ref=dst, send_sem=send.at[k], recv_sem=recv.at[k],
            device_id=device, device_id_type=MESH)
        c.start()
        started.append(c)
        return c

    greet([at.partner(), at.tile(1), at.tile(-1)]
          + [at.along_z(d)[1] for d in range(1, at.nz)]
          + [at.along_y(d)[1] for d in range(1, at.ny)]
          + [at.along_x(d)[1] for d in range(1, at.nx)])

    height = grad.shape[1]
    total = prb.shape[0]
    half = total // 2
    quart = half // 2

    bits = []
    for h in range(2):
        xb = [(b, at.device(at.z, at.y, at.core, to)) for b, to in cube(at.x)]
        yb = [(b, at.device(at.z, to * at.nlo + at.lo, at.core, at.x)) for b, to in cube(at.hi)]
        bits.append((xb if h == 0 else xb[::-1]) + (yb if h == 0 else yb[::-1]))
    cut = [height // 4, height // 8, height // 16, height // 32]
    near = [near1, near2, near3, near4]
    kept = [kept1, kept2, kept3, kept4]

    def object_source(side, h, stage):
        if stage == 0:
            return grad.at[side], h * (height // 2)
        return kept[stage - 1].at[h, side], 0

    def object_send(side, stage):
        out = []
        for h in range(2):
            bit, device = bits[h][stage]
            src, base = object_source(side, h, stage)
            rows = pl.ds(pl.multiple_of(base + (1 - bit) * cut[stage], 8), cut[stage])
            out.append(copy(src.at[rows, :], near[stage].at[h, side], device))
        return out

    def object_add(side, stage, copies):
        for h in range(2):
            copies[h].wait_recv()
            bit, _ = bits[h][stage]
            src, base = object_source(side, h, stage)
            mine = base + bit * cut[stage]

            def add(r, h=h, src=src, mine=mine):
                rows = pl.ds(r, 48)
                kept[stage][h, side, rows, :] = (
                    src[pl.ds(pl.multiple_of(mine + r, 8), 48), :] + near[stage][h, side, rows, :])
            rows_loop(cut[stage], 48, add, unroll=True)

    upd_out = (upd_low, upd_high)

    def object_place(h, stages):
        base = 0
        for stage in range(stages):
            base += bits[h][stage][0] * cut[stage]
        return base

    def object_gather(stage):
        out = []
        for h in range(2):
            rows = pl.ds(pl.multiple_of(object_place(h, stage + 1), 8), cut[stage])
            out.append(copy(upd_out[h].at[rows, :], upd_out[h].at[rows, :], bits[h][stage][1]))
        return out

    crossing = []

    def objects(side):
        o = object_send(side, 0)
        for stage in range(3):
            yield
            object_add(side, stage, o)
            o = object_send(side, stage + 1)
        yield
        object_add(side, 3, o)
        if side == 1:
            crossing.append(copy(kept4.at[:, 1], shifted, at.tile(1)))
            return
        yield
        crossing[0].wait_recv()
        for h in range(2):
            place = object_place(h, 4)

            def finish(r, h=h, place=place):
                rows = pl.ds(r, 48)
                upd_out[h][pl.ds(pl.multiple_of(place + r, 8), 48), :] = object_scale * (
                    kept4[h, 0, rows, :] + shifted[h, rows, :])
            rows_loop(cut[3], 48, finish)
        for stage in (3, 2, 1, 0):
            o = object_gather(stage)
            yield
            for c in o:
                c.wait_recv()

    axes = ((at.along_z, at.along_y, at.nz, at.ny, at.z, at.y),
            (at.along_y, at.along_z, at.ny, at.nz, at.y, at.z))

    def far_first(n):
        return sorted(range(1, n), key=lambda d: (-min(d, n - d), d))

    def share(h, origin, device, part=None):
        n1 = axes[h][2]
        size = quart // n1
        base = my_base + h * quart + lax.rem(origin + n1, n1) * size
        if part is not None:
            size = size // 2
            base += part * size
        rows = pl.ds(pl.multiple_of(base, 8), size)
        return copy(prb_out.at[rows, :], prb_out.at[rows, :], device)

    other_base = (1 - at.core) * half
    my_base = at.core * half
    sub = quart // (at.nz * at.ny)

    def probes():
        def cast_half(r):
            give[pl.ds(r, 32), :] = prb[pl.ds(pl.multiple_of(other_base + r, 8), 32), :].astype(BF16)
        rows_loop(half, 32, cast_half, unroll=4)
        p0 = copy(give, got, at.partner())
        yield
        p0.wait_recv()

        def mix(r):
            rows = pl.ds(r, 32)
            mine = prb[pl.ds(pl.multiple_of(my_base + r, 8), 32), :]
            mixed[rows, :] = (mine + got[rows, :].astype(F32)).astype(BF16)
        rows_loop(half, 32, mix, unroll=4)
        p1 = [[], []]
        for h, (one, _, n1, n2, c1, c2) in enumerate(axes):
            for d in far_first(n1):
                to, device = one(d)
                rows = quart // n1
                src = mixed.at[pl.ds(pl.multiple_of(h * quart + to * rows, 16), rows), :]
                p1[h].append(copy(src, first.at[h, d - 1, pl.ds(0, rows), :], device))
        yield
        p2 = [[], []]
        for h, (_, two, n1, n2, c1, c2) in enumerate(axes):
            rows = quart // n1
            for c in p1[h]:
                c.wait_recv()
            base = h * quart + c1 * rows

            def add_first(r, h=h, n1=n1, base=base):
                acc = (prb[pl.ds(pl.multiple_of(my_base + base + r, 8), 16), :]
                       + got[pl.ds(pl.multiple_of(base + r, 16), 16), :].astype(F32))
                for d in range(n1 - 1):
                    acc += first[h, d, pl.ds(r, 16), :].astype(F32)
                held[h, pl.ds(r, 16), :] = acc
            rows_loop(rows, 16, add_first, unroll=True)
            for d in far_first(n2):
                to, device = two(d)
                src = held.at[h, pl.ds(pl.multiple_of(to * sub, 8), sub), :]
                p2[h].append(copy(src, second.at[h, d - 1], device))
        yield
        for h, (_, _, n1, n2, c1, c2) in enumerate(axes):
            for c in p2[h]:
                c.wait_recv()
            acc = held[h, pl.ds(pl.multiple_of(c2 * sub, 8), sub), :]
            for d in range(n2 - 1):
                acc += second[h, d]
            small[h] = acc
            third[at.x, h] = acc
        p3 = [copy(small, third.at[at.x], at.along_x(d)[1]) for d in far_first(at.nx)]
        yield
        for c in p3:
            c.wait_recv()
        p4 = [[], []]
        for h, (_, two, n1, n2, c1, c2) in enumerate(axes):
            acc = third[0, h]
            for k in range(1, at.nx):
                acc += third[k, h]
            rows = pl.ds(pl.multiple_of(my_base + h * quart + c1 * (quart // n1) + c2 * sub, 8), sub)
            prb_out[rows, :] = probe_scaling * acc
            for d in far_first(n2):
                p4[h].append(copy(prb_out.at[rows, :], prb_out.at[rows, :], two(d)[1]))
        yield
        for h in range(2):
            for c in p4[h]:
                c.wait_recv()
        p6 = []
        steps = max(at.nz, at.ny) // 2

        def ring_send(k, part):
            out = {}
            for h, (one, _, n1, _, c1, _) in enumerate(axes):
                for side in range(2):
                    if 2 * k < n1 or (2 * k == n1 and side == part):
                        ahead = one(1 if side == 0 else n1 - 1)[1]
                        out[h, side] = share(h, c1 - (k - 1) if side == 0 else c1 + (k - 1), ahead, part)
            return out

        ring = [ring_send(1, part) for part in range(2)]
        for h in range(2):
            p6.append(share(h, axes[h][4], at.partner()))
        for k in range(1, steps + 1):
            for part in range(2):
                yield
                for c in ring[part].values():
                    c.wait_recv()
                passed = ring[part]
                ring[part] = ring_send(k + 1, part) if k < steps else {}
                for h, side in passed:
                    p6.append(share(h, axes[h][4] - k if side == 0 else axes[h][4] + k, at.partner(), part))
        yield
        for c in p6:
            c.wait_recv()

    chains = {"r": objects(1), "l": objects(0), "p": probes()}
    for turn in ORDER:
        next(chains[turn], None)
    for c in started:
        c.wait_send()


def sums(sizes, grad, prb, object_scale=1.0, probe_scaling=1.0):
    nz, nlo, nc, nx, nhi = sizes
    ny = nlo * nhi
    height, width = grad.shape[1:]
    total, pw = prb.shape
    half, quart = total // 2, total // 4
    long, short = max(nz, ny), min(nz, ny)
    sub = quart // (nz * ny)
    vmem = pl.BlockSpec(memory_space=pltpu.VMEM)
    stages = []
    for k in (4, 8, 16, 32):
        stages += [pltpu.VMEM((2, 2, height // k, width), F32)] * 2
    return pl.pallas_call(
        functools.partial(sums_kernel, sizes, object_scale, probe_scaling),
        out_shape=(
            jax.ShapeDtypeStruct((height // 2, width), F32),
            jax.ShapeDtypeStruct((height // 2, width), F32),
            jax.ShapeDtypeStruct((total, pw), F32),
        ),
        in_specs=[vmem, vmem],
        out_specs=(vmem, vmem, vmem),
        scratch_shapes=stages + [
            pltpu.VMEM((2, height // 32, width), F32),
            pltpu.VMEM((half, pw), BF16),
            pltpu.VMEM((half, pw), BF16),
            pltpu.VMEM((half, pw), BF16),
            pltpu.VMEM((2, long - 1, quart // short, pw), BF16),
            pltpu.VMEM((2, quart // short, pw), F32),
            pltpu.VMEM((2, long - 1, sub, pw), F32),
            pltpu.VMEM((2, sub, pw), F32),
            pltpu.VMEM((nx, 2, sub, pw), F32),
            pltpu.SemaphoreType.DMA((COPIES,)),
            pltpu.SemaphoreType.DMA((COPIES,)),
        ],
        compiler_params=pltpu.CompilerParams(
            collective_id=1, has_side_effects=True, vmem_limit_bytes=40 << 20),
        name="sums",
    )(grad, prb)


def spread_kernel(sizes, tile, amp, rows, cols, count, halo, amp_got, rows_got, cols_got, count_got, send, recv):
    at = Place(sizes)
    moved = amp_got.shape[0]
    keep = amp.shape[0] - moved
    devices = [at.along_x(d)[1] for d in range(1, moved + 1)]
    greet([at.tile(1), at.tile(-1)] + devices)
    copies = []

    def copy(src, dst, device):
        k = len(copies)
        c = pltpu.make_async_remote_copy(
            src_ref=src, dst_ref=dst, send_sem=send.at[k], recv_sem=recv.at[k],
            device_id=device, device_id_type=MESH)
        c.start()
        copies.append(c)

    copy(tile, halo, at.tile(-1))
    for k, device in enumerate(devices):
        copy(amp.at[keep + k], amp_got.at[k], device)
        copy(rows, rows_got.at[k], device)
        copy(cols, cols_got.at[k], device)
        copy(count, count_got.at[k], device)
    for c in copies:
        c.wait()


def spread(sizes, moved, tile, amp, *meta):
    anywhere = pl.BlockSpec(memory_space=pl.ANY)
    copies = 1 + (1 + len(meta)) * moved
    return pl.pallas_call(
        functools.partial(spread_kernel, sizes),
        out_shape=(
            jax.ShapeDtypeStruct(tile.shape, tile.dtype),
            jax.ShapeDtypeStruct((moved,) + amp.shape[1:], amp.dtype),
        ) + tuple(jax.ShapeDtypeStruct((moved,) + m.shape, m.dtype) for m in meta),
        in_specs=[pl.BlockSpec(memory_space=pltpu.HBM)] * (2 + len(meta)),
        out_specs=(anywhere,) * (2 + len(meta)),
        scratch_shapes=[pltpu.SemaphoreType.DMA((copies,))] * 2,
        compiler_params=pltpu.CompilerParams(
            collective_id=0, has_side_effects=True, vmem_limit_bytes=60 * 1024 * 1024),
        name="spread",
    )(tile, amp, *meta)


def on_device(object_tiles, probe_modes, amplitudes, row_offsets, col_offsets, slot_counts):
    slots = amplitudes.shape[2]
    meta = (row_offsets[0], col_offsets[0], slot_counts)
    halo, amp_got, *meta_got = spread(SIZES, slots - KEEP, object_tiles, amplitudes[0, 0], *meta)
    grad, probe_grad = positions(
        meta, meta_got, object_tiles, halo, probe_modes, amplitudes[0, 0], amp_got,
        dft_tables(probe_modes.shape[2]),
    )
    factor = probe_scale / math.sqrt(lax.axis_size("tile") * lax.axis_size("scan"))
    blocks, _, height, lane = grad.shape
    *update, change = sums(
        SIZES, grad.reshape(2, -1, lane), probe_grad.reshape(-1, probe_modes.shape[3]), object_step, factor)
    update = jnp.concatenate([u.reshape(2, height, lane) for u in update], axis=2)
    new_object = object_tiles + update
    new_probe = probe_modes.astype(F32) + change.reshape(probe_modes.shape)
    return (new_object, new_probe)


def solution(mesh):
    nz, nlo, nc, nx, nhi = SIZES
    if mesh.shape["tile"] != nz * nlo * nc or mesh.shape["scan"] != nx * nhi:
        raise ValueError("other mesh")
    placed = (
        P(None, None, "tile"),
        P(),
        P("tile", "scan", None, None, None),
        P("tile", "scan", None),
        P("tile", "scan", None),
        P("tile", "scan"),
    )
    return jax.shard_map(
        on_device,
        mesh=mesh,
        in_specs=placed,
        out_specs=(P(None, None, "tile"), P()),
        check_vma=False,
    )
```

time: 115 us -> 99.3 us (0.86)
  the two profiles are of different devices: /device:TPU:2 before, /device:TPU:1 now
where the time goes in v3:
time: 99.3 us; the launch traced here: 99 us
  Pallas kernels  91.6 us (92%)
  local copies, waits for them, and re-layouts  3.53 us (4%)
  other arithmetic  2.52 us (3%)
  between operations  1.33 us (1%)
    pallas_call x1, Pallas kernels, sums(): pl.pallas_call(functools.partial(sums_kernel, sizes, object_scale, probe_...  63.7 us
    pallas_call x1, Pallas kernels, spread(): pl.pallas_call(functools.partial(spread_kernel, sizes), out_shape=(jax.Sh...  17 us
    pallas_call x1, Pallas kernels, positions(): pl.pallas_call(positions_kernel, out_shape=(jax.ShapeDtypeStruct((2 * tw...  10.9 us
    unnamed x8, local copies, waits for them, and re-layouts  3.53 us

profile of v3, /device:TPU:1, one launch (start us, length us, event | category | flops | bytes accessed | tf_op | source)
XLA Modules:
  0.0 99.0 jit_solution(6532246437786111948)
XLA Ops:
  1.3 17.0 %spread.1 = (f32[2,384,256]{2,1,0:T(8,128)}, bf16[3,256,256]{2,1,0:T(8,128)(2,1)}, s32[3,1,5]{2,1,0:T(1,128)}, s32[3,1,5]{2,1,0:T(1,128)}, s32[3,1,1]{2,1,0:T(1,128)}) custom-call(f32[2,384,256]{2,1,0:T(8,128)} %tile_in.1, bf16[5,256,256]{2,1,0:T(8,128)(2,1)} %bitcast.13, s32[1,5]{1,0:T(1,128)} %bitcast.15, s32[1,5]{1,0:T(1,128)} %bitcast.17, ...), custom_call_target="tpu_custom_call" | custom-call | tf_op jit(solution)/shard_map/spread/pallas_call | solution.py:592
  18.3 0.0 copy-start.2
  18.3 10.9 %positions.1 = (f32[4,2,384,128]{3,2,1,0:T(8,128)}, f32[2,4,256,256]{3,2,1,0:T(8,128)}) custom-call(s32[1,5]{1,0:T(1,128)} %bitcast.16, s32[1,5]{1,0:T(1,128)} %bitcast.18, s32[1,1]{1,0:T(1,128)S(6)} %copy.9.count.count_own_in, s32[3,1,5]{2,1,0:T(1,128)} %get-tuple-element.12.rows_got_in, s32[3,1,5]{2,1,0:T(1,128)} %get-tuple-element.13.cols_got_in, ...), custom_call_target="tpu_custom_call" | custom-call | tf_op jit(solution)/shard_map/positions/pallas_call | solution.py:216
  29.2 0.0 copy-start
  29.2 1.6 %copy-done = f32[2,4,256,256]{3,2,1,0:T(8,128)S(1)} copy-done((f32[2,4,256,256]{3,2,1,0:T(8,128)S(1)}, f32[2,4,256,256]{3,2,1,0:T(8,128)}, u32[]{:S(2)}) %copy-start) | copy-done | bytes 2097176
  30.8 0.0 copy-start.1
  30.8 1.4 %copy-done.1 = f32[4,2,384,128]{3,2,1,0:T(8,128)S(1)} copy-done((f32[4,2,384,128]{3,2,1,0:T(8,128)S(1)}, f32[4,2,384,128]{3,2,1,0:T(8,128)}, u32[]{:S(2)}) %copy-start.1) | copy-done | bytes 1572888
  32.2 63.7 %sums.1 = (f32[768,128]{1,0:T(8,128)S(1)}, f32[768,128]{1,0:T(8,128)S(1)}, f32[2048,256]{1,0:T(8,128)S(1)}) custom-call(f32[2,1536,128]{2,1,0:T(8,128)S(1)} %bitcast.10, f32[2048,256]{1,0:T(8,128)S(1)} %bitcast.8), custom_call_target="tpu_custom_call" | custom-call | tf_op jit(solution)/shard_map/sums/pallas_call | solution.py:535
  95.9 0.0 copy-start.3
  95.9 0.0 copy-done.2
  95.9 1.0 maximum_add_fusion
  96.9 0.5 copy-done.3
  97.4 1.6 %convert_add_fusion = f32[2,4,256,256]{3,2,1,0:T(8,128)} fusion(f32[2,4,256,256]{3,2,1,0:T(8,128)S(1)} %bitcast.9, bf16[2,4,256,256]{3,2,1,0:T(8,128)(2,1)S(1)} %copy-done.3), kind=kLoop, calls=%fused_computation | loop fusion | flops 1048576 | bytes 5242880 | tf_op jit(solution)/shard_map/add | solution.py:621
Async XLA Ops:
  18.3 77.6 %copy-start.2 = (f32[2,384,256]{2,1,0:T(8,128)S(1)}, f32[2,384,256]{2,1,0:T(8,128)}, u32[]{:S(2)}) copy-start(f32[2,384,256]{2,1,0:T(8,128)} %tile_in.1) | copy-start | bytes 2359300
  29.2 1.6 %copy-start = (f32[2,4,256,256]{3,2,1,0:T(8,128)S(1)}, f32[2,4,256,256]{3,2,1,0:T(8,128)}, u32[]{:S(2)}) copy-start(f32[2,4,256,256]{3,2,1,0:T(8,128)} %get-tuple-element.18) | copy-start | bytes 6291460
  30.8 1.4 %copy-start.1 = (f32[4,2,384,128]{3,2,1,0:T(8,128)S(1)}, f32[4,2,384,128]{3,2,1,0:T(8,128)}, u32[]{:S(2)}) copy-start(f32[4,2,384,128]{3,2,1,0:T(8,128)} %get-tuple-element.17) | copy-start | bytes 4718596
  95.9 1.5 %copy-start.3 = (bf16[2,4,256,256]{3,2,1,0:T(8,128)(2,1)S(1)}, bf16[2,4,256,256]{3,2,1,0:T(8,128)(2,1)}, u32[]{:S(2)}) copy-start(bf16[2,4,256,256]{3,2,1,0:T(8,128)(2,1)} %probe_in.1) | copy-start | bytes 3145732

commit v4 on v3

--- a/solution.py
+++ b/solution.py
@@ -292,13 +292,24 @@
     return ((lax.rem(high + odd, 2), index + 1 - 2 * odd), (high, 3 - index))
 
 
-def sums_kernel(sizes, object_scale, probe_scaling, grad, prb, upd_low, upd_high, prb_out,
+def sums_kernel(sizes, object_scale, probe_scaling, grad_in, prb_in, upd_low, upd_high, prb_out,
+                grad, prb,
                 near1, kept1, near2, kept2, near3, kept3, near4, kept4, shifted,
                 give, got, mixed, first, held, second, small, third,
-                send, recv):
+                send, recv, loaded):
     at = Place(sizes)
     used = [0]
     started = []
+    middle = prb_in.shape[0] // 2
+    theirs = pl.ds(pl.multiple_of((1 - at.core) * middle, 8), middle)
+    ours = pl.ds(pl.multiple_of(at.core * middle, 8), middle)
+    loads = [
+        pltpu.make_async_copy(prb_in.at[theirs, :], prb.at[theirs, :], loaded.at[0]),
+        pltpu.make_async_copy(grad_in, grad, loaded.at[1]),
+        pltpu.make_async_copy(prb_in.at[ours, :], prb.at[ours, :], loaded.at[2]),
+    ]
+    for load in loads:
+        load.start()
 
     def copy(src, dst, device):
         k = used[0]
@@ -338,7 +349,7 @@
         out = []
         for h in range(2):
             bit, device = bits[h][stage]
-            src, base = object_source(side, h, stage)
+            src, base = (grad_in.at[side], h * (height // 2)) if stage == 0 else object_source(side, h, stage)
             rows = pl.ds(pl.multiple_of(base + (1 - bit) * cut[stage], 8), cut[stage])
             out.append(copy(src.at[rows, :], near[stage].at[h, side], device))
         return out
@@ -377,6 +388,8 @@
         o = object_send(side, 0)
         for stage in range(3):
             yield
+            if stage == 0 and side == 1:
+                loads[1].wait()
             object_add(side, stage, o)
             o = object_send(side, stage + 1)
         yield
@@ -421,11 +434,14 @@
     sub = quart // (at.nz * at.ny)
 
     def probes():
+        loads[0].wait()
+
         def cast_half(r):
             give[pl.ds(r, 32), :] = prb[pl.ds(pl.multiple_of(other_base + r, 8), 32), :].astype(BF16)
         rows_loop(half, 32, cast_half, unroll=4)
         p0 = copy(give, got, at.partner())
         yield
+        loads[2].wait()
         p0.wait_recv()
 
         def mix(r):
@@ -539,9 +555,9 @@
             jax.ShapeDtypeStruct((height // 2, width), F32),
             jax.ShapeDtypeStruct((total, pw), F32),
         ),
-        in_specs=[vmem, vmem],
+        in_specs=[pl.BlockSpec(memory_space=pl.ANY)] * 2,
         out_specs=(vmem, vmem, vmem),
-        scratch_shapes=stages + [
+        scratch_shapes=[pltpu.VMEM(grad.shape, F32), pltpu.VMEM(prb.shape, F32)] + stages + [
             pltpu.VMEM((2, height // 32, width), F32),
             pltpu.VMEM((half, pw), BF16),
             pltpu.VMEM((half, pw), BF16),
@@ -553,9 +569,10 @@
             pltpu.VMEM((nx, 2, sub, pw), F32),
             pltpu.SemaphoreType.DMA((COPIES,)),
             pltpu.SemaphoreType.DMA((COPIES,)),
+            pltpu.SemaphoreType.DMA((3,)),
         ],
         compiler_params=pltpu.CompilerParams(
-            collective_id=1, has_side_effects=True, vmem_limit_bytes=40 << 20),
+            collective_id=1, has_side_effects=True, vmem_limit_bytes=52 << 20),
         name="sums",
     )(grad, prb)
 

time: 99.3 us -> 99.3 us (level)
  local copies, waits for them, and re-layouts: 3.53 us -> 0.54 us
  other arithmetic: 2.52 us -> 4.16 us
  Pallas kernels: 91.6 us -> 93 us
    unnamed x8 -> x4, local copies, waits for them, and re-layouts: 3.53 us -> 0.54 us
    add x1, other arithmetic: 1.56 us -> 3.2 us  [on_device(): new_probe = probe_modes.astype(F32) + change.reshape(probe_modes.shape)]
    pallas_call x1, Pallas kernels: 63.7 us -> 65.2 us  [sums(): pl.pallas_call(functools.partial(sums_kernel, sizes, object_scale, probe_...]
where the time goes in v4:
time: 99.3 us; the launch traced here: 99.1 us
  Pallas kernels  93 us (94%)
  other arithmetic  4.16 us (4%)
  between operations  1.32 us (1%)
    pallas_call x1, Pallas kernels, sums(): pl.pallas_call(functools.partial(sums_kernel, sizes, object_scale, probe_...  65.2 us
    pallas_call x1, Pallas kernels, spread(): pl.pallas_call(functools.partial(spread_kernel, sizes), out_shape=(jax.Sh...  17 us
    pallas_call x1, Pallas kernels, positions(): pl.pallas_call(positions_kernel, out_shape=(jax.ShapeDtypeStruct((2 * tw...  10.8 us
    add x1, other arithmetic, on_device(): new_probe = probe_modes.astype(F32) + change.reshape(probe_modes.shape)  3.2 us

profile of v4, /device:TPU:1, one launch (start us, length us, event | category | flops | bytes accessed | tf_op | source)
XLA Modules:
  0.0 99.1 jit_solution(11107729179884780099)
XLA Ops:
  1.3 17.0 %spread.1 = (f32[2,384,256]{2,1,0:T(8,128)}, bf16[3,256,256]{2,1,0:T(8,128)(2,1)}, s32[3,1,5]{2,1,0:T(1,128)}, s32[3,1,5]{2,1,0:T(1,128)}, s32[3,1,1]{2,1,0:T(1,128)}) custom-call(f32[2,384,256]{2,1,0:T(8,128)} %tile_in.1, bf16[5,256,256]{2,1,0:T(8,128)(2,1)} %bitcast.10, s32[1,5]{1,0:T(1,128)} %bitcast.15, s32[1,5]{1,0:T(1,128)} %bitcast.17, ...), custom_call_target="tpu_custom_call" | custom-call | tf_op jit(solution)/shard_map/spread/pallas_call | solution.py:609
  18.3 10.8 %positions.1 = (f32[4,2,384,128]{3,2,1,0:T(8,128)}, f32[2,4,256,256]{3,2,1,0:T(8,128)}) custom-call(s32[1,5]{1,0:T(1,128)} %bitcast.16, s32[1,5]{1,0:T(1,128)} %bitcast.18, s32[1,1]{1,0:T(1,128)S(6)} %copy.9.count.count_own_in, s32[3,1,5]{2,1,0:T(1,128)} %get-tuple-element.12.rows_got_in, s32[3,1,5]{2,1,0:T(1,128)} %get-tuple-element.13.cols_got_in, ...), custom_call_target="tpu_custom_call" | custom-call | tf_op jit(solution)/shard_map/positions/pallas_call | solution.py:216
  29.1 0.0 copy-start
  29.1 65.2 %sums.1 = (f32[768,128]{1,0:T(8,128)S(1)}, f32[768,128]{1,0:T(8,128)S(1)}, f32[2048,256]{1,0:T(8,128)}) custom-call(f32[2,1536,128]{2,1,0:T(8,128)} %bitcast.14, f32[2048,256]{1,0:T(8,128)} %bitcast.12), custom_call_target="tpu_custom_call" | custom-call | tf_op jit(solution)/shard_map/sums/pallas_call | solution.py:551
  94.4 0.0 copy-start.1
  94.4 0.0 copy-done
  94.4 1.0 maximum_add_fusion
  95.3 0.5 copy-done.1
  95.9 3.2 %convert_add_fusion = f32[2,4,256,256]{3,2,1,0:T(8,128)} fusion(f32[2,4,256,256]{3,2,1,0:T(8,128)} %bitcast.13, bf16[2,4,256,256]{3,2,1,0:T(8,128)(2,1)S(1)} %copy-done.1), kind=kLoop, calls=%fused_computation | loop fusion | flops 1048576 | bytes 5242880 | tf_op jit(solution)/shard_map/add | solution.py:638
Async XLA Ops:
  29.1 65.2 %copy-start = (f32[2,384,256]{2,1,0:T(8,128)S(1)}, f32[2,384,256]{2,1,0:T(8,128)}, u32[]{:S(2)}) copy-start(f32[2,384,256]{2,1,0:T(8,128)} %tile_in.1) | copy-start | bytes 2359300
  94.4 1.5 %copy-start.1 = (bf16[2,4,256,256]{3,2,1,0:T(8,128)(2,1)S(1)}, bf16[2,4,256,256]{3,2,1,0:T(8,128)(2,1)}, u32[]{:S(2)}) copy-start(bf16[2,4,256,256]{3,2,1,0:T(8,128)(2,1)} %probe_in.1) | copy-start | bytes 3145732

commit v5 on v3

--- a/solution.py
+++ b/solution.py
@@ -565,7 +565,12 @@
     moved = amp_got.shape[0]
     keep = amp.shape[0] - moved
     devices = [at.along_x(d)[1] for d in range(1, moved + 1)]
-    greet([at.tile(1), at.tile(-1)] + devices)
+    across = jnp.where(at.lo == 0, at.nhi - 1, 1)
+    to_hi = lax.rem(at.hi + jnp.where(at.core == 0, across, 0), at.nhi)
+    from_hi = jnp.where(at.core == 1, lax.rem(at.hi + jnp.where(at.lo == 1, 1, at.nhi - 1), at.nhi), at.hi)
+    beyond = {"tile": at.tile(-1)["tile"], "scan": at.x * at.nhi + to_hi}
+    behind = {"tile": at.tile(1)["tile"], "scan": at.x * at.nhi + from_hi}
+    greet([at.tile(1), at.tile(-1), beyond, behind] + devices)
     copies = []
 
     def copy(src, dst, device):
@@ -576,7 +581,8 @@
         c.start()
         copies.append(c)
 
-    copy(tile, halo, at.tile(-1))
+    copy(tile.at[0], halo.at[0], at.tile(-1))
+    copy(tile.at[1], halo.at[1], beyond)
     for k, device in enumerate(devices):
         copy(amp.at[keep + k], amp_got.at[k], device)
         copy(rows, rows_got.at[k], device)
@@ -588,7 +594,7 @@
 
 def spread(sizes, moved, tile, amp, *meta):
     anywhere = pl.BlockSpec(memory_space=pl.ANY)
-    copies = 1 + (1 + len(meta)) * moved
+    copies = 2 + (1 + len(meta)) * moved
     return pl.pallas_call(
         functools.partial(spread_kernel, sizes),
         out_shape=(

time: 99.3 us -> 98.7 us (level)
    pallas_call x1, Pallas kernels: 17 us -> 14.4 us  [spread(): pl.pallas_call(functools.partial(spread_kernel, sizes), out_shape=(jax.Sh...]
    pallas_call x1, Pallas kernels: 63.7 us -> 65.7 us  [sums(): pl.pallas_call(functools.partial(sums_kernel, sizes, object_scale, probe_...]
where the time goes in v5:
time: 98.7 us; the launch traced here: 98.4 us
  Pallas kernels  91 us (92%)
  local copies, waits for them, and re-layouts  3.53 us (4%)
  other arithmetic  2.52 us (3%)
  between operations  1.33 us (1%)
    pallas_call x1, Pallas kernels, sums(): pl.pallas_call(functools.partial(sums_kernel, sizes, object_scale, probe_...  65.7 us
    pallas_call x1, Pallas kernels, spread(): pl.pallas_call(functools.partial(spread_kernel, sizes), out_shape=(jax.Sh...  14.4 us
    pallas_call x1, Pallas kernels, positions(): pl.pallas_call(positions_kernel, out_shape=(jax.ShapeDtypeStruct((2 * tw...  10.9 us
    unnamed x8, local copies, waits for them, and re-layouts  3.53 us

profile of v5, /device:TPU:1, one launch (start us, length us, event | category | flops | bytes accessed | tf_op | source)
XLA Modules:
  0.0 98.4 jit_solution(12766559351696823126)
XLA Ops:
  1.3 14.4 %spread.1 = (f32[2,384,256]{2,1,0:T(8,128)}, bf16[3,256,256]{2,1,0:T(8,128)(2,1)}, s32[3,1,5]{2,1,0:T(1,128)}, s32[3,1,5]{2,1,0:T(1,128)}, s32[3,1,1]{2,1,0:T(1,128)}) custom-call(f32[2,384,256]{2,1,0:T(8,128)} %tile_in.1, bf16[5,256,256]{2,1,0:T(8,128)(2,1)} %bitcast.13, s32[1,5]{1,0:T(1,128)} %bitcast.15, s32[1,5]{1,0:T(1,128)} %bitcast.17, ...), custom_call_target="tpu_custom_call" | custom-call | tf_op jit(solution)/shard_map/spread/pallas_call | solution.py:598
  15.7 0.0 copy-start.2
  15.7 10.9 %positions.1 = (f32[4,2,384,128]{3,2,1,0:T(8,128)}, f32[2,4,256,256]{3,2,1,0:T(8,128)}) custom-call(s32[1,5]{1,0:T(1,128)} %bitcast.16, s32[1,5]{1,0:T(1,128)} %bitcast.18, s32[1,1]{1,0:T(1,128)S(6)} %copy.9.count.count_own_in, s32[3,1,5]{2,1,0:T(1,128)} %get-tuple-element.12.rows_got_in, s32[3,1,5]{2,1,0:T(1,128)} %get-tuple-element.13.cols_got_in, ...), custom_call_target="tpu_custom_call" | custom-call | tf_op jit(solution)/shard_map/positions/pallas_call | solution.py:216
  26.6 0.0 copy-start
  26.6 1.6 %copy-done = f32[2,4,256,256]{3,2,1,0:T(8,128)S(1)} copy-done((f32[2,4,256,256]{3,2,1,0:T(8,128)S(1)}, f32[2,4,256,256]{3,2,1,0:T(8,128)}, u32[]{:S(2)}) %copy-start) | copy-done | bytes 2097176
  28.2 0.0 copy-start.1
  28.2 1.4 %copy-done.1 = f32[4,2,384,128]{3,2,1,0:T(8,128)S(1)} copy-done((f32[4,2,384,128]{3,2,1,0:T(8,128)S(1)}, f32[4,2,384,128]{3,2,1,0:T(8,128)}, u32[]{:S(2)}) %copy-start.1) | copy-done | bytes 1572888
  29.6 65.7 %sums.1 = (f32[768,128]{1,0:T(8,128)S(1)}, f32[768,128]{1,0:T(8,128)S(1)}, f32[2048,256]{1,0:T(8,128)S(1)}) custom-call(f32[2,1536,128]{2,1,0:T(8,128)S(1)} %bitcast.10, f32[2048,256]{1,0:T(8,128)S(1)} %bitcast.8), custom_call_target="tpu_custom_call" | custom-call | tf_op jit(solution)/shard_map/sums/pallas_call | solution.py:535
  95.3 0.0 copy-start.3
  95.4 0.0 copy-done.2
  95.4 1.0 maximum_add_fusion
  96.3 0.5 copy-done.3
  96.9 1.6 %convert_add_fusion = f32[2,4,256,256]{3,2,1,0:T(8,128)} fusion(f32[2,4,256,256]{3,2,1,0:T(8,128)S(1)} %bitcast.9, bf16[2,4,256,256]{3,2,1,0:T(8,128)(2,1)S(1)} %copy-done.3), kind=kLoop, calls=%fused_computation | loop fusion | flops 1048576 | bytes 5242880 | tf_op jit(solution)/shard_map/add | solution.py:627
Async XLA Ops:
  15.7 79.7 %copy-start.2 = (f32[2,384,256]{2,1,0:T(8,128)S(1)}, f32[2,384,256]{2,1,0:T(8,128)}, u32[]{:S(2)}) copy-start(f32[2,384,256]{2,1,0:T(8,128)} %tile_in.1) | copy-start | bytes 2359300
  26.6 1.6 %copy-start = (f32[2,4,256,256]{3,2,1,0:T(8,128)S(1)}, f32[2,4,256,256]{3,2,1,0:T(8,128)}, u32[]{:S(2)}) copy-start(f32[2,4,256,256]{3,2,1,0:T(8,128)} %get-tuple-element.18) | copy-start | bytes 6291460
  28.2 1.4 %copy-start.1 = (f32[4,2,384,128]{3,2,1,0:T(8,128)S(1)}, f32[4,2,384,128]{3,2,1,0:T(8,128)}, u32[]{:S(2)}) copy-start(f32[4,2,384,128]{3,2,1,0:T(8,128)} %get-tuple-element.17) | copy-start | bytes 4718596
  95.3 1.5 %copy-start.3 = (bf16[2,4,256,256]{3,2,1,0:T(8,128)(2,1)S(1)}, bf16[2,4,256,256]{3,2,1,0:T(8,128)(2,1)}, u32[]{:S(2)}) copy-start(bf16[2,4,256,256]{3,2,1,0:T(8,128)(2,1)} %probe_in.1) | copy-start | bytes 3145732
